TPU v7x, 1024 devices: a whole 4x4x32 slice. The times are simulated.
1024 devices in a mesh: space: 32 (over y, z_hi, core), vel: 32 (over z_lo, x).
Axes of the slice: x: 4, y: 4, z: 32 (z_hi: 4, z_lo: 8; z = z_hi * 8 + z_lo), core: 2. Of those that a mesh axis runs over, the one named last changes fastest.
Arguments:
- phase_density_field: float32 [5, 32, 1024, 1024], P(None, 'vel', 'space'), may hold values from 0.2 to 2.8, as said below
- fourier_scattering_table: float32 [3, 32, 1024], replicated, may hold values from -4 to 4
- odd_stiffness_factor: float32 [5], replicated, may hold values from 0.5 to 8
- electron_bgk_frequency_dt: float32 [2], replicated, may hold values from 0.5 to 4
- electron_kinetic_heat_level: float32 [2], replicated, may hold values from 8 to 24
Outputs:
- next_distribution: float32 [5, 32, 1024, 1024], P(None, 'vel', 'space')
Inputs may be any that keep to these rules, and one draw needn't show every extreme that they name: `phase_density_field`: every entry is positive.
All inputs are finite; a program needn't handle non-finite values.
Results may differ from a plain program's by a relative error of at most 0.0001.
Values sent between devices are 32-bit elements; how exact they have to be, the bound alone decides.
A program may use at most 32 MiB of HBM per device.

v0:
```python
import math

import numpy as np

import jax
import jax.numpy as jnp
from jax import lax
from jax.sharding import PartitionSpec as P

NVX = 32
NVY = 32
NVZ = 32
PAIRS = 1


CFL_NUMBER = 0.2
VELOCITY_STEP = 0.375
COLLIDE_SCALE = 0.25


def extended(x, sides, width):
    for axis, dim in sides:
        devices, length = (lax.axis_size(axis), x.shape[dim])
        up = [(i, (i + 1) % devices) for i in range(devices)]
        down = [(j, i) for i, j in up]
        last = lax.slice_in_dim(x, length - width, length, axis=dim)
        initial = lax.slice_in_dim(x, 0, width, axis=dim)
        before = lax.ppermute(last, axis, up)
        after = lax.ppermute(initial, axis, down)
        x = jnp.concatenate([before, x, after], axis=dim)
    return x


def from_partner(value, axis, stride):
    mask = 2**stride
    pairs = [(source, source ^ mask) for source in range(lax.axis_size(axis))]
    return lax.ppermute(value, axis, pairs)


def velocity_values(indices, extent):
    return (indices.astype(jnp.float32) - (extent - 1) / 2.0) * VELOCITY_STEP


def plane_speed(indices, extent):
    return CFL_NUMBER * (2 * indices - (extent - 1)).astype(jnp.float32) / (extent - 1)


def velocity_index(positions, extent):
    half = extent // 2
    return jnp.where(positions < half, positions, 3 * half - 1 - positions)


def tables(row_index, col_index, extent):
    phases = row_index[:, None] * col_index[None, :] % extent
    angles = phases.astype(jnp.float32) * (2.0 * math.pi / extent)
    return (jnp.cos(angles), jnp.sin(angles))


def multiply(table, operand):
    return jnp.einsum("ka,bam->bkm", table, operand, precision=lax.Precision.HIGHEST)


def rotate(operand, extent_mid, extent_low):
    batch_count, extent_top, merged = operand.shape
    shaped = operand.reshape(batch_count, extent_top, extent_mid, extent_low)
    return jnp.transpose(shaped, (0, 2, 3, 1)).reshape(
        batch_count, extent_mid, extent_low * extent_top
    )


def spectral(real_in, imag_in, orient, real_only):
    extents = (NVX, NVY, NVZ)
    real_now = real_in
    imag_now = imag_in
    for pass_index in range(3):
        extent = extents[pass_index]
        extent_mid = extents[(pass_index + 1) % 3]
        extent_low = extents[(pass_index + 2) % 3]
        plain = jnp.arange(extent, dtype=jnp.int32)
        if pass_index == 0 and orient < 0:
            cosines, sines = tables(plain, velocity_index(plain, extent), extent)
        elif pass_index == 0:
            cosines, sines = tables(velocity_index(plain, extent), plain, extent)
        else:
            cosines, sines = tables(plain, plain, extent)
        final_pass = real_only and pass_index == 2
        if imag_now is None:
            real_next = multiply(cosines, real_now)
            imag_next = orient * multiply(sines, real_now)
        else:
            real_next = multiply(cosines, real_now) - orient * multiply(sines, imag_now)
            if final_pass:
                imag_next = None
            else:
                imag_next = multiply(cosines, imag_now) + orient * multiply(sines, real_now)
        real_now = rotate(real_next, extent_mid, extent_low)
        imag_now = None if imag_next is None else rotate(imag_next, extent_mid, extent_low)
    return (real_now, imag_now)


def collide(heavy_block, fourier_scattering_table):
    species_count, x_extent_size, cell_count, merged = heavy_block.shape
    flattened = jnp.transpose(heavy_block, (0, 2, 1, 3)).reshape(
        species_count * cell_count, x_extent_size, merged
    )
    spec_real, spec_imag = spectral(flattened, None, -1, False)

    def invert(kernel_index):
        kernel = fourier_scattering_table[kernel_index][None, :, :]
        real_out, unused = spectral(spec_real * kernel, spec_imag * kernel, 1, True)
        return real_out / (NVX * NVY * NVZ)

    gain_sum = invert(0) * invert(1)
    loss_term = flattened * invert(2 * PAIRS)
    updated = flattened + COLLIDE_SCALE * (gain_sum - loss_term)
    return jnp.transpose(
        updated.reshape(species_count, cell_count, x_extent_size, merged), (0, 2, 1, 3)
    )


def split_bf16(values):
    rounded = lax.reduce_precision(values, exponent_bits=8, mantissa_bits=7)
    return rounded.astype(jnp.bfloat16), (values - rounded).astype(jnp.bfloat16)


def kron_tables(extent):
    size = extent * extent
    index = np.arange(size)
    phases = (
        np.outer(index // extent, index // extent) + np.outer(index % extent, index % extent)
    ) % extent
    angles = phases * (2.0 * np.pi / extent)

    def split(values):
        high = values.astype(jnp.bfloat16)
        low = (values - high.astype(np.float64)).astype(jnp.bfloat16)
        return jnp.asarray(high), jnp.asarray(low)

    return split(np.cos(angles)), split(np.sin(angles))


def split_dot(operand, table):
    high, low = table
    op_high, op_low = split_bf16(operand)

    def dot(left, right):
        return jnp.dot(left, right, preferred_element_type=jnp.float32)

    return dot(op_high, high) + (dot(op_low, high) + dot(op_high, low))


def collide_kron(heavy_block, fourier_scattering_table):
    species_count, x_extent_size, cell_count, merged = heavy_block.shape
    hp = lax.Precision.HIGHEST
    flat = jnp.transpose(heavy_block, (0, 2, 1, 3)).reshape(
        species_count * cell_count, x_extent_size, merged
    )
    plain = jnp.arange(x_extent_size, dtype=jnp.int32)
    x_cos, x_sin = tables(plain, velocity_index(plain, x_extent_size), x_extent_size)
    wide_cos, wide_sin = kron_tables(NVY)
    rows = species_count * cell_count
    x_real = jnp.einsum("kp,bpm->kbm", x_cos, flat, precision=hp)
    x_imag = -jnp.einsum("kp,bpm->kbm", x_sin, flat, precision=hp)
    stacked = jnp.concatenate([x_real, x_imag], axis=1).reshape(-1, merged)
    by_cos = split_dot(stacked, wide_cos).reshape(x_extent_size, 2, rows, merged)
    by_sin = split_dot(stacked, wide_sin).reshape(x_extent_size, 2, rows, merged)
    spec_real = by_cos[:, 0] + by_sin[:, 1]
    spec_imag = by_cos[:, 1] - by_sin[:, 0]
    kernels = jnp.transpose(fourier_scattering_table, (1, 0, 2))[:, :, None, :]
    z_real = kernels * spec_real[:, None]
    z_imag = kernels * spec_imag[:, None]
    u_real = jnp.einsum("kp,kqbm->pqbm", x_cos, z_real, precision=hp) - jnp.einsum(
        "kp,kqbm->pqbm", x_sin, z_imag, precision=hp
    )
    u_imag = jnp.einsum("kp,kqbm->pqbm", x_sin, z_real, precision=hp) + jnp.einsum(
        "kp,kqbm->pqbm", x_cos, z_imag, precision=hp
    )
    parts = (
        split_dot(u_real.reshape(-1, merged), wide_cos)
        - split_dot(u_imag.reshape(-1, merged), wide_sin)
    ).reshape(
        x_extent_size, fourier_scattering_table.shape[0], rows, merged
    ) / (NVX * NVY * NVZ)
    fields = jnp.transpose(flat, (1, 0, 2))
    updated = fields + COLLIDE_SCALE * (parts[:, 0] * parts[:, 1] - fields * parts[:, 2])
    return jnp.transpose(
        updated.reshape(x_extent_size, species_count, cell_count, merged), (1, 0, 2, 3)
    )


def advance(padded, mirror, odd_stiffness_factor, leading_plane, x_extent_size):
    planes = padded.shape[1]
    positions = leading_plane + jnp.arange(planes, dtype=jnp.int32)
    speeds = plane_speed(velocity_index(positions, x_extent_size), x_extent_size)[
        None, :, None, None
    ]
    even_part = 0.5 * (padded + mirror)
    odd_part = 0.5 * (padded - mirror)
    even_diff = 0.5 * (even_part[:, :, 2:] - even_part[:, :, :-2])
    odd_diff = 0.5 * (odd_part[:, :, 2:] - odd_part[:, :, :-2])
    even_new = even_part[:, :, 1:-1] - speeds * odd_diff
    odd_new = (odd_part[:, :, 1:-1] - speeds * even_diff) / (1.0 + odd_stiffness_factor)[
        :, None, None, None
    ]
    return even_new + odd_new


def moments(light_portion, leading_plane, x_extent_size):
    planes = light_portion.shape[1]
    positions = leading_plane + jnp.arange(planes, dtype=jnp.int32)
    along_first = velocity_values(velocity_index(positions, x_extent_size), x_extent_size)
    along_second = jnp.repeat(velocity_values(jnp.arange(NVY, dtype=jnp.int32), NVY), NVZ)
    along_third = jnp.tile(velocity_values(jnp.arange(NVZ, dtype=jnp.int32), NVZ), NVY)
    density = jnp.sum(light_portion, axis=(1, 3))
    moment_first = jnp.sum(light_portion * along_first[None, :, None, None], axis=(1, 3))
    moment_second = jnp.sum(light_portion * along_second, axis=(1, 3))
    moment_third = jnp.sum(light_portion * along_third, axis=(1, 3))
    return jnp.stack([density, moment_first, moment_second, moment_third])


def relax_light_species(
    light_portion,
    summed_moments,
    leading_plane,
    x_extent_size,
    electron_bgk_frequency_dt,
    electron_kinetic_heat_level,
):
    light_count, planes, cell_count, merged = light_portion.shape
    density = summed_moments[0]
    drifts = summed_moments[1:] / density[None]
    equilibrium_heat_level = electron_kinetic_heat_level[:, None, None]

    def integration_coefficient(values, drift):
        offset_counts_per_row = values[None, None, :] - drift[:, :, None]
        return jnp.exp(
            -(offset_counts_per_row * offset_counts_per_row) / (2.0 * equilibrium_heat_level)
        )

    def profile(values, drift):
        weights = integration_coefficient(values, drift)
        return weights / jnp.sum(weights, axis=2, keepdims=True)

    full_first = integration_coefficient(
        velocity_values(jnp.arange(x_extent_size, dtype=jnp.int32), x_extent_size), drifts[0]
    )
    positions = leading_plane + jnp.arange(planes, dtype=jnp.int32)
    local_values = velocity_values(velocity_index(positions, x_extent_size), x_extent_size)
    local_first = integration_coefficient(local_values, drifts[0]) / jnp.sum(
        full_first, axis=2, keepdims=True
    )
    grid_second = velocity_values(jnp.arange(NVY, dtype=jnp.int32), NVY)
    grid_third = velocity_values(jnp.arange(NVZ, dtype=jnp.int32), NVZ)
    profile_rest = (
        profile(grid_second, drifts[1])[:, :, :, None]
        * profile(grid_third, drifts[2])[:, :, None, :]
    ).reshape(light_count, cell_count, merged)
    maxwell = (
        density[:, None, :, None]
        * jnp.transpose(local_first, (0, 2, 1))[:, :, :, None]
        * profile_rest[:, None, :, :]
    )
    rates = electron_bgk_frequency_dt[:, None, None, None]
    return (light_portion + rates * maxwell) / (1.0 + rates)


def body(
    phase_density_field,
    fourier_scattering_table,
    odd_stiffness_factor,
    electron_bgk_frequency_dt,
    electron_kinetic_heat_level,
):
    species_count = phase_density_field.shape[0]
    heavy_count = species_count - electron_bgk_frequency_dt.shape[0]
    x_extent_size = fourier_scattering_table.shape[1]
    planes = phase_density_field.shape[1]
    padded = extended(phase_density_field, (("space", 2),), 1)
    leading_plane = lax.axis_index("vel") * planes
    positions = leading_plane + jnp.arange(planes, dtype=jnp.int32)
    speeds = plane_speed(velocity_index(positions, x_extent_size), x_extent_size)[
        None, :, None, None
    ]
    shifted = phase_density_field - speeds * (
        0.5 * (padded[:, :, 2:] - padded[:, :, :-2])
    )
    gathered = lax.all_to_all(shifted, "vel", split_axis=2, concat_axis=1, tiled=True)
    half = x_extent_size // 2
    mirror = jnp.flip(
        jnp.concatenate([gathered[:, half:], gathered[:, :half]], axis=1), axis=3
    )
    ratio = 1.0 / (1.0 + odd_stiffness_factor)
    alpha = (0.5 * (1.0 + ratio))[:, None, None, None]
    beta = (0.5 * (1.0 - ratio))[:, None, None, None]
    advanced = alpha * gathered + beta * mirror
    heavy_part = collide_kron(advanced[:heavy_count], fourier_scattering_table)
    light_portion = advanced[heavy_count:]
    summed_moments = moments(light_portion, 0, x_extent_size)
    light_portion = relax_light_species(
        light_portion,
        summed_moments,
        0,
        x_extent_size,
        electron_bgk_frequency_dt,
        electron_kinetic_heat_level,
    )
    result = jnp.concatenate([heavy_part, light_portion], axis=0)
    return lax.all_to_all(result, "vel", split_axis=1, concat_axis=2, tiled=True)


def solution(mesh):
    in_specs = (P(None, "vel", "space", None), P(), P(), P(), P())
    out_specs = P(None, "vel", "space", None)
    return jax.shard_map(body, mesh=mesh, in_specs=in_specs, out_specs=out_specs, check_vma=False)
```

profile of v0, /device:TPU:24, one launch (start us, length us, event | category | flops | bytes accessed | tf_op | source)
XLA Modules:
  0.0 170.7 jit_solution(2006362951712960689)
XLA Ops:
  0.0 1.0 fusion.103
  1.0 22.6 %collective-permute-start = (f32[5,1,1,1024]{3,2,1,0:T(1,128)S(1)}, f32[5,1,1,1024]{3,2,1,0:T(1,128)S(1)}, u32[]{:S(2)}, u32[]{:S(2)}) collective-permute-start(f32[5,1,1,1024]{3,2,1,0:T(1,128)S(1)} %get-tuple-element.21), channel_id=1, source_target_pairs={{32,0},{64,32},{96,64},{128,96},{160,128},{192,160},{224,192},{256... | collective-permute-start | bytes 61448 | tf_op jit(solution)/shard_map/ppermute | solution.py:29
  23.7 1.9 %collective-permute-start.1 = (f32[5,1,1,1024]{3,2,1,0:T(1,128)S(1)}, f32[5,1,1,1024]{3,2,1,0:T(1,128)S(1)}, u32[]{:S(2)}, u32[]{:S(2)}) collective-permute-start(f32[5,1,1,1024]{3,2,1,0:T(1,128)S(1)} %get-tuple-element.22), channel_id=1, source_target_pairs={{0,32},{32,64},{64,96},{96,128},{128,160},{160,192},{192,224},{224... | collective-permute-start | bytes 61448 | tf_op jit(solution)/shard_map/ppermute | solution.py:28
  25.6 12.8 %collective-permute-done.1 = f32[5,1,1,1024]{3,2,1,0:T(1,128)S(1)} collective-permute-done((f32[5,1,1,1024]{3,2,1,0:T(1,128)S(1)}, f32[5,1,1,1024]{3,2,1,0:T(1,128)S(1)}, u32[]{:S(2)}, u32[]{:S(2)}) %collective-permute-start.1) | collective-permute-done | bytes 20512 | tf_op jit(solution)/shard_map/ppermute | solution.py:28
  38.4 1.8 %fusion.25 = f32[5,1,32,1024]{3,2,1,0:T(8,128)S(1)} fusion(f32[5,1,32,1024]{3,2,1,0:T(8,128)} %param.9, f32[5,1,1,1024]{3,2,1,0:T(1,128)S(1)} %collective-permute-done.1, f32[5,1,1,1024]{3,2,1,0:T(1,128)S(1)} %collective-permute-done, f32[]{:T(128)} %bitcast.1), kind=kLoop, calls=%fused_computation.34 | loop fusion | flops 819200 | bytes 1351684 | tf_op jit(solution)/shard_map/sub | solution.py:284
  40.2 1.5 copy.110
  41.7 7.9 %all-to-all-start = ((f32[5,1,32,1024]{3,1,0,2:T(1,128)}), f32[5,1,32,1024]{3,1,0,2:T(1,128)S(1)}, u32[]{:S(2)}, u32[]{:S(2)}) async-start(f32[5,1,32,1024]{3,1,0,2:T(1,128)} %copy.110), calls=%async_computation | async-start | bytes 1310720 | tf_op jit(solution)/shard_map/all_to_all | solution.py:287
  49.9 24.1 %all-to-all-done = f32[5,1,32,1024]{3,1,0,2:T(1,128)S(1)} async-done(((f32[5,1,32,1024]{3,1,0,2:T(1,128)}), f32[5,1,32,1024]{3,1,0,2:T(1,128)S(1)}, u32[]{:S(2)}, u32[]{:S(2)}) %all-to-all-start) | async-done | bytes 655392 | tf_op jit(solution)/shard_map/all_to_all | solution.py:287
  76.8 1.5 copy.114
  78.3 1.5 reshape.697
  80.2 1.5 fusion.53
  81.6 1.5 fusion.105
  85.5 1.5 fusion.19
  86.9 2.5 %reshape.698 = f32[32,2,3,1024]{3,2,1,0:T(4,128)} reshape(f32[192,1024]{1,0:T(8,128)} %fusion.19) | data formatting | bytes 1572864 | tf_op jit(solution)/shard_map/reshape | solution.py:165
  89.4 3.3 %fusion.18 = f32[192,1024]{1,0:T(8,128)} fusion(f32[192,1024]{1,0:T(8,128)} %fusion.105, f32[192,1024]{1,0:T(8,128)S(1)} %copy-done.16, bf16[192,1024]{1,0:T(8,128)(2,1)S(1)} %reduce-precision_convert_fusion.2, bf16[1024,1024]{1,0:T(8,128)(2,1)} %constant.73.clone), kind=kOutput, calls=%fused_computation.21 | convolution fusion | flops 403046400 | bytes 4849664 | tf_op jit(solution)/shard_map/dot_general | solution.py:147
  92.7 2.4 %reshape.699 = f32[32,2,3,1024]{3,2,1,0:T(4,128)} reshape(f32[192,1024]{1,0:T(8,128)} %fusion.18) | data formatting | bytes 1572864 | tf_op jit(solution)/shard_map/reshape | solution.py:166
  95.1 1.6 fusion.39
  97.7 2.3 %fusion = f32[32,3,3,1024]{3,0,2,1:T(8,128)} fusion(f32[32,3,1024]{2,0,1:T(8,128)S(1)} %copy.116, f32[32,3,1024]{2,0,1:T(8,128)S(1)} %bitcast.90, s32[32]{0:T(128)S(1)} %compare_select_fusion), kind=kOutput, calls=%fused_computation.4 | convolution fusion | flops 113555456 | bytes 1966208 | tf_op jit(solution)/shard_map/kp,kqbm->pqbm/dot_general | solution.py:175
  99.9 1.2 fusion.2
  102.2 1.2 fusion.8
  103.4 2.0 %copy.117 = f32[32,3,3,1024]{3,2,1,0:T(4,128)} copy(f32[32,3,3,1024]{3,0,2,1:T(8,128)S(1)} %fusion.8) | data formatting | bytes 2359296 | tf_op jit(solution)/shard_map/sub | solution.py:172
  105.4 1.9 %reshape.700 = f32[288,1024]{1,0:T(8,128)S(1)} reshape(f32[32,3,3,1024]{3,2,1,0:T(4,128)} %copy.117) | data formatting | bytes 2359296 | tf_op jit(solution)/shard_map/reshape | solution.py:179
  107.4 3.5 %fusion.36 = f32[288,1024]{1,0:T(8,128)} fusion(bf16[1024,1024]{1,0:T(8,128)(2,1)} %constant.70.clone, f32[288,1024]{1,0:T(8,128)S(1)} %reshape.700), kind=kOutput, calls=%fused_computation.50 | convolution fusion | flops 604864512 | bytes 4456448 | tf_op jit(solution)/shard_map/dot_general | solution.py:147
  110.9 1.8 %fusion.51 = f32[288,1024]{1,0:T(8,128)} fusion(bf16[1024,1024]{1,0:T(8,128)(2,1)S(1)} %copy-done.2, f32[288,1024]{1,0:T(8,128)S(1)} %reshape.700), kind=kOutput, calls=%fused_computation.72 | convolution fusion | flops 604569600 | bytes 4456448 | tf_op jit(solution)/shard_map/dot_general | solution.py:147
  112.7 1.2 fusion.11
  114.0 2.0 %copy.118 = f32[32,3,3,1024]{3,2,1,0:T(4,128)} copy(f32[32,3,3,1024]{3,0,2,1:T(8,128)S(1)} %fusion.11) | data formatting | bytes 2359296 | tf_op jit(solution)/shard_map/add | solution.py:175
  115.9 2.5 %reshape.701 = f32[288,1024]{1,0:T(8,128)} reshape(f32[32,3,3,1024]{3,2,1,0:T(4,128)} %copy.118) | data formatting | bytes 2359296 | tf_op jit(solution)/shard_map/reshape | solution.py:180
  118.5 3.2 %fusion.34 = f32[288,1024]{1,0:T(8,128)} fusion(bf16[1024,1024]{1,0:T(8,128)(2,1)S(1)} %copy-done, f32[288,1024]{1,0:T(8,128)} %reshape.701), kind=kOutput, calls=%fused_computation.49 | convolution fusion | flops 604864512 | bytes 4456448 | tf_op jit(solution)/shard_map/dot_general | solution.py:147
  121.7 1.8 %fusion.52 = f32[288,1024]{1,0:T(8,128)} fusion(bf16[1024,1024]{1,0:T(8,128)(2,1)S(1)} %copy-done, f32[288,1024]{1,0:T(8,128)S(1)} %copy-done.3), kind=kOutput, calls=%fused_computation.73 | convolution fusion | flops 604569600 | bytes 4456448 | tf_op jit(solution)/shard_map/dot_general | solution.py:147
  123.5 1.1 slice_reduce_fusion
  125.2 3.2 %fusion.16 = f32[288,1024]{1,0:T(8,128)S(1)} fusion(f32[288,1024]{1,0:T(8,128)} %fusion.51, f32[288,1024]{1,0:T(8,128)} %fusion.36, bf16[1024,1024]{1,0:T(8,128)(2,1)} %constant.71.clone, f32[288,1024]{1,0:T(8,128)S(1)} %reshape.700), kind=kOutput, calls=%fused_computation.18 | convolution fusion | flops 605159424 | bytes 6815744 | tf_op jit(solution)/shard_map/dot_general | solution.py:147
  133.1 36.6 %all_to_all.24 = f32[5,32,1,1024]{3,2,0,1:T(1,128)S(1)} all-to-all(f32[5,32,1,1024]{3,2,0,1:T(1,128)S(1)} %copy.122), channel_id=1, replica_groups=mesh['space'=32,'vel'=32] {'vel'}, dimensions={1} | all-to-all | bytes 1310720 | tf_op jit(solution)/shard_map/all_to_all | solution.py:308
  (80 shorter events, 13.8 us)
Async XLA Ops:
  1.0 24.6 %collective-permute-start = (f32[5,1,1,1024]{3,2,1,0:T(1,128)S(1)}, f32[5,1,1,1024]{3,2,1,0:T(1,128)S(1)}, u32[]{:S(2)}, u32[]{:S(2)}) collective-permute-start(f32[5,1,1,1024]{3,2,1,0:T(1,128)S(1)} %get-tuple-element.21), channel_id=1, source_target_pairs={{32,0},{64,32},{96,64},{128,96},{160,128},{192,160},{224,192},{256... | collective-permute-start | bytes 61448 | tf_op jit(solution)/shard_map/ppermute | solution.py:29
  23.7 14.7 %collective-permute-start.1 = (f32[5,1,1,1024]{3,2,1,0:T(1,128)S(1)}, f32[5,1,1,1024]{3,2,1,0:T(1,128)S(1)}, u32[]{:S(2)}, u32[]{:S(2)}) collective-permute-start(f32[5,1,1,1024]{3,2,1,0:T(1,128)S(1)} %get-tuple-element.22), channel_id=1, source_target_pairs={{0,32},{32,64},{64,96},{96,128},{128,160},{160,192},{192,224},{224... | collective-permute-start | bytes 61448 | tf_op jit(solution)/shard_map/ppermute | solution.py:28
  40.1 9.7 %copy-start.19 = (f32[2]{0:T(128)S(1)}, f32[2]{0:T(128)}, u32[]{:S(2)}) copy-start(f32[2]{0:T(128)} %param.13) | copy-start | bytes 28
  40.2 9.7 %copy-start.18 = (f32[2]{0:T(128)S(1)}, f32[2]{0:T(128)}, u32[]{:S(2)}) copy-start(f32[2]{0:T(128)} %param.12) | copy-start | bytes 28
  40.2 9.7 %copy-start.20 = (f32[5]{0:T(128)S(1)}, f32[5]{0:T(128)}, u32[]{:S(2)}) copy-start(f32[5]{0:T(128)} %param.11) | copy-start | bytes 64
  41.7 32.3 %all-to-all-start = ((f32[5,1,32,1024]{3,1,0,2:T(1,128)}), f32[5,1,32,1024]{3,1,0,2:T(1,128)S(1)}, u32[]{:S(2)}, u32[]{:S(2)}) async-start(f32[5,1,32,1024]{3,1,0,2:T(1,128)} %copy.110), calls=%async_computation | async-start | bytes 1310720 | tf_op jit(solution)/shard_map/all_to_all | solution.py:287
  75.3 1.4 copy-start.5
  78.2 1.9 %copy-start = (bf16[1024,1024]{1,0:T(8,128)(2,1)S(1)}, bf16[1024,1024]{1,0:T(8,128)(2,1)}, u32[]{:S(2)}) copy-start(bf16[1024,1024]{1,0:T(8,128)(2,1)} %constant.72.clone) | copy-start | bytes 6291460
  81.6 1.7 copy-start.1
  83.9 1.6 copy-start.7
  86.9 2.5 %copy-start.16 = (f32[192,1024]{1,0:T(8,128)S(1)}, f32[192,1024]{1,0:T(8,128)}, u32[]{:S(2)}) copy-start(f32[192,1024]{1,0:T(8,128)} %fusion.53) | copy-start | bytes 2359300
  92.7 2.4 %copy-start.13 = (f32[32,2,3,1024]{3,2,1,0:T(4,128)S(1)}, f32[32,2,3,1024]{3,2,1,0:T(4,128)}, u32[]{:S(2)}) copy-start(f32[32,2,3,1024]{3,2,1,0:T(4,128)} %reshape.698) | copy-start | bytes 2359300
  96.7 1.0 copy-start.10
  101.4 0.8 copy-start.14
  107.4 3.6 %copy-start.2 = (bf16[1024,1024]{1,0:T(8,128)(2,1)S(1)}, bf16[1024,1024]{1,0:T(8,128)(2,1)}, u32[]{:S(2)}) copy-start(bf16[1024,1024]{1,0:T(8,128)(2,1)} %constant.70.clone) | copy-start | bytes 6291460
  110.9 1.8 %copy-start.11 = (f32[3,32,1024]{2,1,0:T(8,128)S(1)}, f32[3,32,1024]{2,1,0:T(8,128)}, u32[]{:S(2)}) copy-start(f32[3,32,1024]{2,1,0:T(8,128)} %param.10) | copy-start | bytes 1179652
  110.9 1.8 %copy-start.12 = (f32[32,3,3,1024]{3,0,2,1:T(8,128)S(1)}, f32[32,3,3,1024]{3,0,2,1:T(8,128)}, u32[]{:S(2)}) copy-start(f32[32,3,3,1024]{3,0,2,1:T(8,128)} %fusion) | copy-start | bytes 3538948
  110.9 1.8 %copy-start.15 = (f32[32,3,1024]{2,0,1:T(8,128)S(1)}, f32[32,3,1024]{2,0,1:T(8,128)}, u32[]{:S(2)}) copy-start(f32[32,3,1024]{2,0,1:T(8,128)} %copy-done.14) | copy-start | bytes 1179652
  118.5 3.2 %copy-start.3 = (f32[288,1024]{1,0:T(8,128)S(1)}, f32[288,1024]{1,0:T(8,128)}, u32[]{:S(2)}) copy-start(f32[288,1024]{1,0:T(8,128)} %reshape.701) | copy-start | bytes 3538948
  125.2 3.3 %copy-start.4 = (f32[288,1024]{1,0:T(8,128)S(1)}, f32[288,1024]{1,0:T(8,128)}, u32[]{:S(2)}) copy-start(f32[288,1024]{1,0:T(8,128)} %reshape.701) | copy-start | bytes 3538948
  125.2 3.3 %copy-start.8 = (bf16[1024,1024]{1,0:T(8,128)(2,1)S(1)}, bf16[1024,1024]{1,0:T(8,128)(2,1)}, u32[]{:S(2)}) copy-start(bf16[1024,1024]{1,0:T(8,128)(2,1)} %constant.73.clone) | copy-start | bytes 6291460
  125.2 3.6 %copy-start.9 = (f32[288,1024]{1,0:T(8,128)S(1)}, f32[288,1024]{1,0:T(8,128)}, u32[]{:S(2)}) copy-start(f32[288,1024]{1,0:T(8,128)} %fusion.52) | copy-start | bytes 3538948
  125.2 3.9 %copy-start.17 = (f32[288,1024]{1,0:T(8,128)S(1)}, f32[288,1024]{1,0:T(8,128)}, u32[]{:S(2)}) copy-start(f32[288,1024]{1,0:T(8,128)} %fusion.34) | copy-start | bytes 3538948
  130.5 1.1 copy-start.6
where the time goes:
time: 172 us; the launch traced here: 171 us
  waiting for transfers between devices  36.9 us (21%)
  blocking collectives  36.6 us (21%)
  starting transfers between devices  32.4 us (19%)
  matrix products  30.5 us (18%)
  local copies, waits for them, and re-layouts  27.6 us (16%)
  other arithmetic  6.18 us (4%)
    all_to_all x1, blocking collectives, body(): lax.all_to_all(result, 'vel', split_axis=1, concat_axis=2, tiled=True)  36.6 us
    all_to_all x1, waiting for transfers between devices, body(): lax.all_to_all(shifted, 'vel', split_axis=2, concat_axis=1, tiled=True)  24.1 us
    dot_general x12, matrix products, dot(): return jnp.dot(left, right, preferred_element_type=jnp.float32)  23.2 us
    ppermute x1, starting transfers between devices, extended(): after = lax.ppermute(initial, axis, down)  22.6 us
    ppermute x1, waiting for transfers between devices, extended(): before = lax.ppermute(last, axis, up)  12.8 us
    all_to_all x1, starting transfers between devices, body(): lax.all_to_all(shifted, 'vel', split_axis=2, concat_axis=1, tiled=True)  7.87 us
    unnamed x42, local copies, waits for them, and re-layouts  4.6 us
  transfers between devices with their start and end apart: 3, of which 2 were waited for; matrix products, arithmetic and copies ran while one was open for 0% of the time, Pallas kernels for 0%

commit v1 on v0

--- a/solution.py
+++ b/solution.py
@@ -146,7 +146,9 @@
     def dot(left, right):
         return jnp.dot(left, right, preferred_element_type=jnp.float32)
 
-    return dot(op_high, high) + (dot(op_low, high) + dot(op_high, low))
+    count = operand.shape[0]
+    by_high = dot(jnp.concatenate([op_high, op_low], axis=0), high)
+    return by_high[:count] + (by_high[count:] + dot(op_high, low))
 
 
 def collide_kron(heavy_block, fourier_scattering_table):

time: 172 us -> 174 us (1.012)
  the two profiles are of different devices: /device:TPU:24 before, /device:TPU:1 now
where the time goes in v1:
time: 174 us
  blocking collectives  39.8 us (23%)
  waiting for transfers between devices  38 us (22%)
  starting transfers between devices  33.8 us (19%)
  local copies, waits for them, and re-layouts  25.1 us (14%)
  matrix products  24.5 us (14%)
  other arithmetic  12.1 us (7%)
    all_to_all x1, blocking collectives, body(): lax.all_to_all(result, 'vel', split_axis=1, concat_axis=2, tiled=True)  39.8 us
    all_to_all x1, waiting for transfers between devices, body(): lax.all_to_all(shifted, 'vel', split_axis=2, concat_axis=1, tiled=True)  26.1 us
    ppermute x1, starting transfers between devices, extended(): before = lax.ppermute(last, axis, up)  16.8 us
    all_to_all x1, starting transfers between devices, body(): lax.all_to_all(shifted, 'vel', split_axis=2, concat_axis=1, tiled=True)  15.1 us
    dot_general x8, matrix products, dot(): return jnp.dot(left, right, preferred_element_type=jnp.float32)  14.9 us
    ppermute x1, waiting for transfers between devices, extended(): after = lax.ppermute(initial, axis, down)  11.9 us
  transfers between devices with their start and end apart: 3, of which 2 were waited for; matrix products, arithmetic and copies ran while one was open for 1% of the time, Pallas kernels for 0%

profile of v1, /device:TPU:1, one launch (start us, length us, event | category | flops | bytes accessed | tf_op | source)
XLA Modules:
  0.0 173.7 jit_solution(9456372926962716665)
XLA Ops:
  0.0 1.0 fusion.107
  1.0 16.8 %collective-permute-start.1 = (f32[5,1,1,1024]{3,2,1,0:T(1,128)S(1)}, f32[5,1,1,1024]{3,2,1,0:T(1,128)S(1)}, u32[]{:S(2)}, u32[]{:S(2)}) collective-permute-start(f32[5,1,1,1024]{3,2,1,0:T(1,128)S(1)} %get-tuple-element.28), channel_id=1, source_target_pairs={{0,32},{32,64},{64,96},{96,128},{128,160},{160,192},{192,224},{224... | collective-permute-start | bytes 61448 | tf_op jit(solution)/shard_map/ppermute | solution.py:28
  17.9 1.9 %collective-permute-start = (f32[5,1,1,1024]{3,2,1,0:T(1,128)S(1)}, f32[5,1,1,1024]{3,2,1,0:T(1,128)S(1)}, u32[]{:S(2)}, u32[]{:S(2)}) collective-permute-start(f32[5,1,1,1024]{3,2,1,0:T(1,128)S(1)} %get-tuple-element.27), channel_id=1, source_target_pairs={{32,0},{64,32},{96,64},{128,96},{160,128},{192,160},{224,192},{256... | collective-permute-start | bytes 61448 | tf_op jit(solution)/shard_map/ppermute | solution.py:29
  19.8 11.9 %collective-permute-done = f32[5,1,1,1024]{3,2,1,0:T(1,128)S(1)} collective-permute-done((f32[5,1,1,1024]{3,2,1,0:T(1,128)S(1)}, f32[5,1,1,1024]{3,2,1,0:T(1,128)S(1)}, u32[]{:S(2)}, u32[]{:S(2)}) %collective-permute-start) | collective-permute-done | bytes 20512 | tf_op jit(solution)/shard_map/ppermute | solution.py:29
  31.7 1.9 %fusion.33 = f32[5,1,32,1024]{3,2,1,0:T(8,128)S(1)} fusion(f32[5,1,32,1024]{3,2,1,0:T(8,128)} %param.9, f32[5,1,1,1024]{3,2,1,0:T(1,128)S(1)} %collective-permute-done.1, f32[5,1,1,1024]{3,2,1,0:T(1,128)S(1)} %collective-permute-done, f32[]{:T(128)} %bitcast.1), kind=kLoop, calls=%fused_computation.43 | loop fusion | flops 819200 | bytes 1351684 | tf_op jit(solution)/shard_map/sub | solution.py:286
  33.6 1.5 copy.110
  35.1 15.1 %all-to-all-start = ((f32[5,1,32,1024]{3,1,0,2:T(1,128)}), f32[5,1,32,1024]{3,1,0,2:T(1,128)S(1)}, u32[]{:S(2)}, u32[]{:S(2)}) async-start(f32[5,1,32,1024]{3,1,0,2:T(1,128)} %copy.110), calls=%async_computation | async-start | bytes 1310720 | tf_op jit(solution)/shard_map/all_to_all | solution.py:289
  52.2 26.1 %all-to-all-done = f32[5,1,32,1024]{3,1,0,2:T(1,128)S(1)} async-done(((f32[5,1,32,1024]{3,1,0,2:T(1,128)}), f32[5,1,32,1024]{3,1,0,2:T(1,128)S(1)}, u32[]{:S(2)}, u32[]{:S(2)}) %all-to-all-start) | async-done | bytes 655392 | tf_op jit(solution)/shard_map/all_to_all | solution.py:289
  81.8 2.7 %fusion.44 = f32[384,1024]{1,0:T(8,128)S(1)} fusion(bf16[1024,1024]{1,0:T(8,128)(2,1)} %constant.72.clone, bf16[192,1024]{1,0:T(8,128)(2,1)S(1)} %get-tuple-element.23, bf16[192,1024]{1,0:T(8,128)(2,1)S(1)} %get-tuple-element.24), kind=kOutput, calls=%fused_computation.62 | convolution fusion | flops 806879232 | bytes 4456448 | tf_op jit(solution)/shard_map/dot_general | solution.py:147
  84.5 1.5 fusion.18
  86.0 2.3 %reshape.699 = f32[32,2,3,1024]{3,2,1,0:T(4,128)} reshape(f32[192,1024]{1,0:T(8,128)} %fusion.18) | data formatting | bytes 1572864 | tf_op jit(solution)/shard_map/reshape | solution.py:168
  88.3 2.7 %fusion.45 = f32[384,1024]{1,0:T(8,128)S(1)} fusion(bf16[1024,1024]{1,0:T(8,128)(2,1)} %constant.70.clone, bf16[192,1024]{1,0:T(8,128)(2,1)S(1)} %get-tuple-element.23, bf16[192,1024]{1,0:T(8,128)(2,1)S(1)} %get-tuple-element.24), kind=kOutput, calls=%fused_computation.63 | convolution fusion | flops 806879232 | bytes 4456448 | tf_op jit(solution)/shard_map/dot_general | solution.py:147
  91.1 1.5 fusion.19
  92.6 2.3 %reshape.698 = f32[32,2,3,1024]{3,2,1,0:T(4,128)} reshape(f32[192,1024]{1,0:T(8,128)} %fusion.19) | data formatting | bytes 1572864 | tf_op jit(solution)/shard_map/reshape | solution.py:167
  94.9 2.7 %fusion.43 = (f32[32,3,1024]{2,1,0:T(4,128)}, f32[32,3,1024]{2,1,0:T(4,128)S(1)}) fusion(f32[32,2,3,1024]{3,2,1,0:T(4,128)} %reshape.699, f32[32,2,3,1024]{3,2,1,0:T(4,128)} %reshape.698), kind=kLoop, calls=%fused_computation.61 | loop fusion | flops 196608 | bytes 2359296 | tf_op jit(solution)/shard_map/mul | solution.py:172
  98.6 2.3 %fusion.2 = f32[32,3,3,1024]{3,0,2,1:T(8,128)} fusion(f32[32,3,1024]{2,0,1:T(8,128)S(1)} %copy.116, f32[32,3,1024]{2,0,1:T(8,128)S(1)} %bitcast.86, s32[32]{0:T(128)S(1)} %compare_select_fusion), kind=kOutput, calls=%fused_computation.6 | convolution fusion | flops 113555456 | bytes 1966208 | tf_op jit(solution)/shard_map/kp,kqbm->pqbm/dot_general | solution.py:174
  100.8 2.2 %fusion = f32[32,3,3,1024]{3,0,2,1:T(8,128)} fusion(f32[32,3,1024]{2,0,1:T(8,128)S(1)} %copy.116, f32[32,3,1024]{2,0,1:T(8,128)S(1)} %bitcast.87, s32[32]{0:T(128)S(1)} %compare_select_fusion), kind=kOutput, calls=%fused_computation.4 | convolution fusion | flops 113555456 | bytes 1966208 | tf_op jit(solution)/shard_map/kp,kqbm->pqbm/dot_general | solution.py:177
  104.4 1.3 copy.115
  105.7 2.5 %fusion.8 = f32[32,3,3,1024]{3,0,2,1:T(8,128)S(1)} fusion(f32[32,3,3,1024]{3,0,2,1:T(8,128)} %fusion.2, f32[32,3,1024]{2,0,1:T(8,128)S(1)} %copy.115, f32[32,3,1024]{2,0,1:T(8,128)S(1)} %bitcast.88, s32[32]{0:T(128)S(1)} %compare_select_fusion), kind=kOutput, calls=%fused_computation.12 | convolution fusion | flops 113850368 | bytes 3145856 | tf_op jit(solution)/shard_map/kp,kqbm->pqbm/dot_general | solution.py:174
  108.2 2.0 %copy.117 = f32[32,3,3,1024]{3,2,1,0:T(4,128)} copy(f32[32,3,3,1024]{3,0,2,1:T(8,128)S(1)} %fusion.8) | data formatting | bytes 2359296 | tf_op jit(solution)/shard_map/sub | solution.py:174
  110.2 2.6 %reshape.700 = f32[288,1024]{1,0:T(8,128)} reshape(f32[32,3,3,1024]{3,2,1,0:T(4,128)} %copy.117) | data formatting | bytes 2359296 | tf_op jit(solution)/shard_map/reshape | solution.py:181
  112.8 1.6 fusion.20
  114.7 1.4 fusion.22
  116.3 1.8 %fusion.16 = f32[288,1024]{1,0:T(8,128)} fusion(bf16[288,1024]{1,0:T(8,128)(2,1)S(1)} %get-tuple-element.22, bf16[1024,1024]{1,0:T(8,128)(2,1)S(1)} %copy-done.4, f32[576,1024]{1,0:T(8,128)S(1)} %fusion.22), kind=kOutput, calls=%fused_computation.18 | convolution fusion | flops 604569600 | bytes 6225920 | tf_op jit(solution)/shard_map/dot_general | solution.py:147
  118.1 1.2 fusion.11
  119.3 2.0 %copy.118 = f32[32,3,3,1024]{3,2,1,0:T(4,128)} copy(f32[32,3,3,1024]{3,0,2,1:T(8,128)S(1)} %fusion.11) | data formatting | bytes 2359296 | tf_op jit(solution)/shard_map/add | solution.py:177
  121.3 2.6 %reshape.701 = f32[288,1024]{1,0:T(8,128)} reshape(f32[32,3,3,1024]{3,2,1,0:T(4,128)} %copy.118) | data formatting | bytes 2359296 | tf_op jit(solution)/shard_map/reshape | solution.py:182
  123.9 1.6 fusion.21
  125.8 1.4 fusion.26
  127.2 1.9 %fusion.17 = f32[288,1024]{1,0:T(8,128)} fusion(f32[288,1024]{1,0:T(8,128)S(1)} %copy-done.5, bf16[288,1024]{1,0:T(8,128)(2,1)S(1)} %get-tuple-element.20, bf16[1024,1024]{1,0:T(8,128)(2,1)S(1)} %copy-done, f32[576,1024]{1,0:T(8,128)S(1)} %fusion.26), kind=kOutput, calls=%fused_computation.19 | convolution fusion | flops 605159424 | bytes 7405568 | tf_op jit(solution)/shard_map/dot_general | solution.py:147
  129.1 1.6 div.155
  132.9 39.8 %all_to_all.24 = f32[5,32,1,1024]{3,2,0,1:T(1,128)S(1)} all-to-all(f32[5,32,1,1024]{3,2,0,1:T(1,128)S(1)} %copy.122), channel_id=1, replica_groups=mesh['space'=32,'vel'=32] {'vel'}, dimensions={1} | all-to-all | bytes 1310720 | tf_op jit(solution)/shard_map/all_to_all | solution.py:310
  (68 shorter events, 11.6 us)
Async XLA Ops:
  1.0 18.8 %collective-permute-start.1 = (f32[5,1,1,1024]{3,2,1,0:T(1,128)S(1)}, f32[5,1,1,1024]{3,2,1,0:T(1,128)S(1)}, u32[]{:S(2)}, u32[]{:S(2)}) collective-permute-start(f32[5,1,1,1024]{3,2,1,0:T(1,128)S(1)} %get-tuple-element.28), channel_id=1, source_target_pairs={{0,32},{32,64},{64,96},{96,128},{128,160},{160,192},{192,224},{224... | collective-permute-start | bytes 61448 | tf_op jit(solution)/shard_map/ppermute | solution.py:28
  17.9 13.8 %collective-permute-start = (f32[5,1,1,1024]{3,2,1,0:T(1,128)S(1)}, f32[5,1,1,1024]{3,2,1,0:T(1,128)S(1)}, u32[]{:S(2)}, u32[]{:S(2)}) collective-permute-start(f32[5,1,1,1024]{3,2,1,0:T(1,128)S(1)} %get-tuple-element.27), channel_id=1, source_target_pairs={{32,0},{64,32},{96,64},{128,96},{160,128},{192,160},{224,192},{256... | collective-permute-start | bytes 61448 | tf_op jit(solution)/shard_map/ppermute | solution.py:29
  33.6 17.5 %copy-start.12 = (f32[5]{0:T(128)S(1)}, f32[5]{0:T(128)}, u32[]{:S(2)}) copy-start(f32[5]{0:T(128)} %param.11) | copy-start | bytes 64
  33.6 17.5 %copy-start.9 = (f32[2]{0:T(128)S(1)}, f32[2]{0:T(128)}, u32[]{:S(2)}) copy-start(f32[2]{0:T(128)} %param.12) | copy-start | bytes 28
  33.6 18.0 %copy-start.13 = (f32[2]{0:T(128)S(1)}, f32[2]{0:T(128)}, u32[]{:S(2)}) copy-start(f32[2]{0:T(128)} %param.13) | copy-start | bytes 28
  35.1 43.2 %all-to-all-start = ((f32[5,1,32,1024]{3,1,0,2:T(1,128)}), f32[5,1,32,1024]{3,1,0,2:T(1,128)S(1)}, u32[]{:S(2)}, u32[]{:S(2)}) async-start(f32[5,1,32,1024]{3,1,0,2:T(1,128)} %copy.110), calls=%async_computation | async-start | bytes 1310720 | tf_op jit(solution)/shard_map/all_to_all | solution.py:289
  81.8 2.7 %copy-start = (bf16[1024,1024]{1,0:T(8,128)(2,1)S(1)}, bf16[1024,1024]{1,0:T(8,128)(2,1)}, u32[]{:S(2)}) copy-start(bf16[1024,1024]{1,0:T(8,128)(2,1)} %constant.73.clone) | copy-start | bytes 6291460
  88.3 2.7 %copy-start.3 = (bf16[1024,1024]{1,0:T(8,128)(2,1)S(1)}, bf16[1024,1024]{1,0:T(8,128)(2,1)}, u32[]{:S(2)}) copy-start(bf16[1024,1024]{1,0:T(8,128)(2,1)} %constant.71.clone) | copy-start | bytes 6291460
  97.6 1.0 copy-start.1
  100.8 2.3 %copy-start.7 = (f32[32]{0:T(128)S(1)}, f32[32]{0:T(128)}, u32[]{:S(2)}) copy-start(f32[32]{0:T(128)} %get-tuple-element.36) | copy-start | bytes 388
  100.8 2.5 %copy-start.8 = (f32[2]{0:T(128)S(1)}, f32[2]{0:T(128)}, u32[]{:S(2)}) copy-start(f32[2]{0:T(128)} %broadcast_multiply_fusion.1) | copy-start | bytes 28
  112.8 1.9 %copy-start.15 = (bf16[1024,1024]{1,0:T(8,128)(2,1)S(1)}, bf16[1024,1024]{1,0:T(8,128)(2,1)}, u32[]{:S(2)}) copy-start(bf16[1024,1024]{1,0:T(8,128)(2,1)} %constant.70.clone) | copy-start | bytes 6291460
  114.7 1.6 copy-start.4
  116.3 1.8 %copy-start.2 = (f32[32,3,3,1024]{3,0,2,1:T(8,128)S(1)}, f32[32,3,3,1024]{3,0,2,1:T(8,128)}, u32[]{:S(2)}) copy-start(f32[32,3,3,1024]{3,0,2,1:T(8,128)} %fusion) | copy-start | bytes 3538948
  123.9 1.9 %copy-start.14 = (bf16[1024,1024]{1,0:T(8,128)(2,1)S(1)}, bf16[1024,1024]{1,0:T(8,128)(2,1)}, u32[]{:S(2)}) copy-start(bf16[1024,1024]{1,0:T(8,128)(2,1)} %constant.72.clone) | copy-start | bytes 6291460
  125.8 1.4 copy-start.5
  130.7 0.7 copy-start.6
  130.7 0.7 copy-start.10
  130.7 0.7 copy-start.11

commit v2 on v0

--- a/solution.py
+++ b/solution.py
@@ -284,17 +284,21 @@
     shifted = phase_density_field - speeds * (
         0.5 * (padded[:, :, 2:] - padded[:, :, :-2])
     )
-    gathered = lax.all_to_all(shifted, "vel", split_axis=2, concat_axis=1, tiled=True)
     half = x_extent_size // 2
-    mirror = jnp.flip(
-        jnp.concatenate([gathered[:, half:], gathered[:, :half]], axis=1), axis=3
-    )
     ratio = 1.0 / (1.0 + odd_stiffness_factor)
     alpha = (0.5 * (1.0 + ratio))[:, None, None, None]
     beta = (0.5 * (1.0 - ratio))[:, None, None, None]
-    advanced = alpha * gathered + beta * mirror
-    heavy_part = collide_kron(advanced[:heavy_count], fourier_scattering_table)
-    light_portion = advanced[heavy_count:]
+
+    def gather_advance(first, last):
+        gathered = lax.all_to_all(
+            shifted[first:last], "vel", split_axis=2, concat_axis=1, tiled=True
+        )
+        mirror = jnp.flip(
+            jnp.concatenate([gathered[:, half:], gathered[:, :half]], axis=1), axis=3
+        )
+        return alpha[first:last] * gathered + beta[first:last] * mirror
+
+    light_portion = gather_advance(heavy_count, species_count)
     summed_moments = moments(light_portion, 0, x_extent_size)
     light_portion = relax_light_species(
         light_portion,
@@ -304,8 +308,10 @@
         electron_bgk_frequency_dt,
         electron_kinetic_heat_level,
     )
-    result = jnp.concatenate([heavy_part, light_portion], axis=0)
-    return lax.all_to_all(result, "vel", split_axis=1, concat_axis=2, tiled=True)
+    light_back = lax.all_to_all(light_portion, "vel", split_axis=1, concat_axis=2, tiled=True)
+    heavy_part = collide_kron(gather_advance(0, heavy_count), fourier_scattering_table)
+    heavy_back = lax.all_to_all(heavy_part, "vel", split_axis=1, concat_axis=2, tiled=True)
+    return jnp.concatenate([heavy_back, light_back], axis=0)
 
 
 def solution(mesh):

time: 172 us -> 191 us (1.11)
  the two profiles are of different devices: /device:TPU:24 before, /device:TPU:32 now
where the time goes in v2:
time: 191 us; the launch traced here: 190 us
  starting transfers between devices  64.6 us (34%)
  waiting for transfers between devices  59.9 us (31%)
  local copies, waits for them, and re-layouts  30.8 us (16%)
  matrix products  26.3 us (14%)
  other arithmetic  7.67 us (4%)
    all_to_all x2, waiting for transfers between devices, gather_advance(): lax.all_to_all(shifted[first:last], 'vel', split_axis=2, concat_axis=1, t...  30 us
    ppermute x1, starting transfers between devices, extended(): after = lax.ppermute(initial, axis, down)  24 us
    dot_general x12, matrix products, dot(): return jnp.dot(left, right, preferred_element_type=jnp.float32)  19 us
    all_to_all x2, starting transfers between devices, gather_advance(): lax.all_to_all(shifted[first:last], 'vel', split_axis=2, concat_axis=1, t...  18.5 us
    all_to_all x1, waiting for transfers between devices, body(): lax.all_to_all(heavy_part, 'vel', split_axis=1, concat_axis=2, tiled=True)  15.6 us
    ppermute x1, waiting for transfers between devices, extended(): before = lax.ppermute(last, axis, up)  14.3 us
    all_to_all x1, starting transfers between devices, body(): lax.all_to_all(heavy_part, 'vel', split_axis=1, concat_axis=2, tiled=True)  12.6 us
    unnamed x39, local copies, waits for them, and re-layouts  7.79 us
  transfers between devices with their start and end apart: 6, of which 4 were waited for; matrix products, arithmetic and copies ran while one was open for 28% of the time, Pallas kernels for 0%

profile of v2, /device:TPU:32, one launch (start us, length us, event | category | flops | bytes accessed | tf_op | source)
XLA Modules:
  0.0 189.8 jit_solution(10835365826799517475)
XLA Ops:
  0.0 1.8 copy.116
  1.8 24.0 %collective-permute-start = (f32[5,1,1,1024]{3,1,0,2:T(1,128)S(1)}, f32[5,1,1,1024]{3,1,0,2:T(1,128)S(1)}, u32[]{:S(2)}, u32[]{:S(2)}) collective-permute-start(f32[5,1,1,1024]{3,1,0,2:T(1,128)S(1)} %get-tuple-element.20), channel_id=1, source_target_pairs={{32,0},{64,32},{96,64},{128,96},{160,128},{192,160},{224,192},{256... | collective-permute-start | bytes 61448 | tf_op jit(solution)/shard_map/ppermute | solution.py:29
  25.8 1.9 %collective-permute-start.1 = (f32[5,1,1,1024]{3,1,0,2:T(1,128)S(1)}, f32[5,1,1,1024]{3,1,0,2:T(1,128)S(1)}, u32[]{:S(2)}, u32[]{:S(2)}) collective-permute-start(f32[5,1,1,1024]{3,1,0,2:T(1,128)S(1)} %get-tuple-element.21), channel_id=1, source_target_pairs={{0,32},{32,64},{64,96},{96,128},{128,160},{160,192},{192,224},{224... | collective-permute-start | bytes 61448 | tf_op jit(solution)/shard_map/ppermute | solution.py:28
  27.7 14.3 %collective-permute-done.1 = f32[5,1,1,1024]{3,1,0,2:T(1,128)S(1)} collective-permute-done((f32[5,1,1,1024]{3,1,0,2:T(1,128)S(1)}, f32[5,1,1,1024]{3,1,0,2:T(1,128)S(1)}, u32[]{:S(2)}, u32[]{:S(2)}) %collective-permute-start.1) | collective-permute-done | bytes 20512 | tf_op jit(solution)/shard_map/ppermute | solution.py:28
  42.0 1.8 multiply_subtract_fusion
  44.7 8.5 %all-to-all-start.2 = ((f32[2,1,32,1024]{3,0,1,2:T(2,128)}), f32[2,1,32,1024]{3,0,1,2:T(2,128)S(1)}, u32[]{:S(2)}, u32[]{:S(2)}) async-start(f32[2,1,32,1024]{3,0,1,2:T(2,128)} %copy.130), calls=%async_computation.2 | async-start | bytes 524288 | tf_op jit(solution)/shard_map/all_to_all | solution.py:293
  53.9 13.2 %all-to-all-done.2 = f32[2,1,32,1024]{3,0,1,2:T(2,128)S(1)} async-done(((f32[2,1,32,1024]{3,0,1,2:T(2,128)}), f32[2,1,32,1024]{3,0,1,2:T(2,128)S(1)}, u32[]{:S(2)}, u32[]{:S(2)}) %all-to-all-start.2) | async-done | bytes 262176 | tf_op jit(solution)/shard_map/all_to_all | solution.py:293
  67.1 10.0 %all-to-all-start = ((f32[3,1,32,1024]{3,1,0,2:T(1,128)}), f32[3,1,32,1024]{3,1,0,2:T(1,128)S(1)}, u32[]{:S(2)}, u32[]{:S(2)}) async-start(f32[3,1,32,1024]{3,1,0,2:T(1,128)} %slice.105), calls=%async_computation | async-start | bytes 786432 | tf_op jit(solution)/shard_map/all_to_all | solution.py:293
  81.4 16.8 %all-to-all-done = f32[3,1,32,1024]{3,1,0,2:T(1,128)S(1)} async-done(((f32[3,1,32,1024]{3,1,0,2:T(1,128)}), f32[3,1,32,1024]{3,1,0,2:T(1,128)S(1)}, u32[]{:S(2)}, u32[]{:S(2)}) %all-to-all-start) | async-done | bytes 393248 | tf_op jit(solution)/shard_map/all_to_all | solution.py:293
  98.2 7.7 %all-to-all-start.3 = ((f32[2,32,1,1024]{3,0,2,1:T(2,128)}), f32[2,32,1,1024]{3,0,2,1:T(2,128)}, u32[]{:S(2)}, u32[]{:S(2)}) async-start(f32[2,32,1,1024]{3,0,2,1:T(2,128)} %divide_bitcast_fusion), calls=%async_computation.3 | async-start | bytes 524288 | tf_op jit(solution)/shard_map/all_to_all | solution.py:311
  108.4 1.5 copy.120
  109.9 1.5 reshape.725
  111.8 1.5 fusion.49
  113.3 1.5 fusion.103
  117.1 1.5 fusion.19
  118.6 1.5 reshape.726
  120.1 3.5 %fusion.18 = f32[192,1024]{1,0:T(8,128)} fusion(f32[192,1024]{1,0:T(8,128)} %fusion.103, f32[192,1024]{1,0:T(8,128)} %fusion.49, bf16[192,1024]{1,0:T(8,128)(2,1)S(1)} %reduce-precision_convert_fusion.2, bf16[1024,1024]{1,0:T(8,128)(2,1)} %constant.73.clone), kind=kOutput, calls=%fused_computation.21 | convolution fusion | flops 403046400 | bytes 4849664 | tf_op jit(solution)/shard_map/dot_general | solution.py:147
  123.6 2.3 %reshape.727 = f32[32,2,3,1024]{3,2,1,0:T(4,128)} reshape(f32[192,1024]{1,0:T(8,128)} %fusion.18) | data formatting | bytes 1572864 | tf_op jit(solution)/shard_map/reshape | solution.py:166
  125.9 1.6 fusion.37
  128.5 2.2 %fusion = f32[32,3,3,1024]{3,0,2,1:T(8,128)} fusion(f32[32,3,1024]{2,0,1:T(8,128)S(1)} %copy.122, f32[32,3,1024]{2,0,1:T(8,128)S(1)} %bitcast.100, s32[32]{0:T(128)S(1)} %compare_select_fusion), kind=kOutput, calls=%fused_computation.4 | convolution fusion | flops 113555456 | bytes 1966208 | tf_op jit(solution)/shard_map/kp,kqbm->pqbm/dot_general | solution.py:175
  130.7 1.2 fusion.2
  132.9 1.2 fusion.8
  134.2 2.0 %copy.123 = f32[32,3,3,1024]{3,2,1,0:T(4,128)} copy(f32[32,3,3,1024]{3,0,2,1:T(8,128)S(1)} %fusion.8) | data formatting | bytes 2359296 | tf_op jit(solution)/shard_map/sub | solution.py:172
  136.2 2.0 %reshape.728 = f32[288,1024]{1,0:T(8,128)S(1)} reshape(f32[32,3,3,1024]{3,2,1,0:T(4,128)} %copy.123) | data formatting | bytes 2359296 | tf_op jit(solution)/shard_map/reshape | solution.py:179
  138.2 3.5 %fusion.34 = f32[288,1024]{1,0:T(8,128)} fusion(bf16[1024,1024]{1,0:T(8,128)(2,1)} %constant.70.clone, f32[288,1024]{1,0:T(8,128)S(1)} %reshape.728), kind=kOutput, calls=%fused_computation.45 | convolution fusion | flops 604864512 | bytes 4456448 | tf_op jit(solution)/shard_map/dot_general | solution.py:147
  141.7 1.8 fusion.47
  143.6 1.2 fusion.11
  144.8 2.0 %copy.124 = f32[32,3,3,1024]{3,2,1,0:T(4,128)} copy(f32[32,3,3,1024]{3,0,2,1:T(8,128)S(1)} %fusion.11) | data formatting | bytes 2359296 | tf_op jit(solution)/shard_map/add | solution.py:175
  146.8 2.6 %reshape.729 = f32[288,1024]{1,0:T(8,128)} reshape(f32[32,3,3,1024]{3,2,1,0:T(4,128)} %copy.124) | data formatting | bytes 2359296 | tf_op jit(solution)/shard_map/reshape | solution.py:180
  149.3 2.1 %fusion.32 = f32[288,1024]{1,0:T(8,128)S(1)} fusion(bf16[1024,1024]{1,0:T(8,128)(2,1)S(1)} %copy-done, f32[288,1024]{1,0:T(8,128)} %reshape.729), kind=kOutput, calls=%fused_computation.44 | convolution fusion | flops 604864512 | bytes 4456448 | tf_op jit(solution)/shard_map/dot_general | solution.py:147
  159.6 12.6 %all-to-all-start.1 = ((f32[3,32,1,1024]{3,2,0,1:T(1,128)}), f32[3,32,1,1024]{3,2,0,1:T(1,128)S(1)}, u32[]{:S(2)}, u32[]{:S(2)}) async-start(f32[3,32,1,1024]{3,2,0,1:T(1,128)} %copy.128), calls=%async_computation.1 | async-start | bytes 786432 | tf_op jit(solution)/shard_map/all_to_all | solution.py:313
  173.2 15.6 %all-to-all-done.1 = f32[3,32,1,1024]{3,2,0,1:T(1,128)S(1)} async-done(((f32[3,32,1,1024]{3,2,0,1:T(1,128)}), f32[3,32,1,1024]{3,2,0,1:T(1,128)S(1)}, u32[]{:S(2)}, u32[]{:S(2)}) %all-to-all-start.1) | async-done | bytes 393248 | tf_op jit(solution)/shard_map/all_to_all | solution.py:313
  (91 shorter events, 23.0 us)
Async XLA Ops:
  1.8 25.9 %collective-permute-start = (f32[5,1,1,1024]{3,1,0,2:T(1,128)S(1)}, f32[5,1,1,1024]{3,1,0,2:T(1,128)S(1)}, u32[]{:S(2)}, u32[]{:S(2)}) collective-permute-start(f32[5,1,1,1024]{3,1,0,2:T(1,128)S(1)} %get-tuple-element.20), channel_id=1, source_target_pairs={{32,0},{64,32},{96,64},{128,96},{160,128},{192,160},{224,192},{256... | collective-permute-start | bytes 61448 | tf_op jit(solution)/shard_map/ppermute | solution.py:29
  25.8 16.2 %collective-permute-start.1 = (f32[5,1,1,1024]{3,1,0,2:T(1,128)S(1)}, f32[5,1,1,1024]{3,1,0,2:T(1,128)S(1)}, u32[]{:S(2)}, u32[]{:S(2)}) collective-permute-start(f32[5,1,1,1024]{3,1,0,2:T(1,128)S(1)} %get-tuple-element.21), channel_id=1, source_target_pairs={{0,32},{32,64},{64,96},{96,128},{128,160},{160,192},{192,224},{224... | collective-permute-start | bytes 61448 | tf_op jit(solution)/shard_map/ppermute | solution.py:28
  44.6 32.5 %copy-start.17 = (f32[5]{0:T(128)S(1)}, f32[5]{0:T(128)}, u32[]{:S(2)}) copy-start(f32[5]{0:T(128)} %param.11) | copy-start | bytes 64
  44.6 32.9 %copy-start.18 = (f32[2]{0:T(128)S(1)}, f32[2]{0:T(128)}, u32[]{:S(2)}) copy-start(f32[2]{0:T(128)} %param.13) | copy-start | bytes 28
  44.6 32.9 %copy-start.16 = (f32[2]{0:T(128)S(1)}, f32[2]{0:T(128)}, u32[]{:S(2)}) copy-start(f32[2]{0:T(128)} %param.12) | copy-start | bytes 28
  44.7 22.4 %all-to-all-start.2 = ((f32[2,1,32,1024]{3,0,1,2:T(2,128)}), f32[2,1,32,1024]{3,0,1,2:T(2,128)S(1)}, u32[]{:S(2)}, u32[]{:S(2)}) async-start(f32[2,1,32,1024]{3,0,1,2:T(2,128)} %copy.130), calls=%async_computation.2 | async-start | bytes 524288 | tf_op jit(solution)/shard_map/all_to_all | solution.py:293
  67.1 31.1 %all-to-all-start = ((f32[3,1,32,1024]{3,1,0,2:T(1,128)}), f32[3,1,32,1024]{3,1,0,2:T(1,128)S(1)}, u32[]{:S(2)}, u32[]{:S(2)}) async-start(f32[3,1,32,1024]{3,1,0,2:T(1,128)} %slice.105), calls=%async_computation | async-start | bytes 786432 | tf_op jit(solution)/shard_map/all_to_all | solution.py:293
  98.2 61.4 %all-to-all-start.3 = ((f32[2,32,1,1024]{3,0,2,1:T(2,128)}), f32[2,32,1,1024]{3,0,2,1:T(2,128)}, u32[]{:S(2)}, u32[]{:S(2)}) async-start(f32[2,32,1,1024]{3,0,2,1:T(2,128)} %divide_bitcast_fusion), calls=%async_computation.3 | async-start | bytes 524288 | tf_op jit(solution)/shard_map/all_to_all | solution.py:311
  106.9 0.8 copy-start.8
  109.9 1.9 %copy-start = (bf16[1024,1024]{1,0:T(8,128)(2,1)S(1)}, bf16[1024,1024]{1,0:T(8,128)(2,1)}, u32[]{:S(2)}) copy-start(bf16[1024,1024]{1,0:T(8,128)(2,1)} %constant.72.clone) | copy-start | bytes 6291460
  113.3 1.7 copy-start.1
  115.5 1.6 copy-start.5
  127.5 1.0 copy-start.10
  132.2 0.7 copy-start.14
  138.2 3.6 %copy-start.2 = (bf16[1024,1024]{1,0:T(8,128)(2,1)S(1)}, bf16[1024,1024]{1,0:T(8,128)(2,1)}, u32[]{:S(2)}) copy-start(bf16[1024,1024]{1,0:T(8,128)(2,1)} %constant.70.clone) | copy-start | bytes 6291460
  141.7 1.8 copy-start.11
  141.7 1.8 copy-start.12
  141.7 1.8 copy-start.15
  149.3 2.1 %copy-start.3 = (f32[288,1024]{1,0:T(8,128)S(1)}, f32[288,1024]{1,0:T(8,128)}, u32[]{:S(2)}) copy-start(f32[288,1024]{1,0:T(8,128)} %reshape.729) | copy-start | bytes 3538948
  151.5 1.3 copy-start.4
  151.5 2.0 %copy-start.6 = (bf16[1024,1024]{1,0:T(8,128)(2,1)S(1)}, bf16[1024,1024]{1,0:T(8,128)(2,1)}, u32[]{:S(2)}) copy-start(bf16[1024,1024]{1,0:T(8,128)(2,1)} %constant.71.clone) | copy-start | bytes 6291460
  151.5 2.2 %copy-start.13 = (f32[288,1024]{1,0:T(8,128)S(1)}, f32[288,1024]{1,0:T(8,128)}, u32[]{:S(2)}) copy-start(f32[288,1024]{1,0:T(8,128)} %fusion.34) | copy-start | bytes 3538948
  153.8 1.6 copy-start.7
  156.7 1.0 copy-start.9
  159.6 29.2 %all-to-all-start.1 = ((f32[3,32,1,1024]{3,2,0,1:T(1,128)}), f32[3,32,1,1024]{3,2,0,1:T(1,128)S(1)}, u32[]{:S(2)}, u32[]{:S(2)}) async-start(f32[3,32,1,1024]{3,2,0,1:T(1,128)} %copy.128), calls=%async_computation.1 | async-start | bytes 786432 | tf_op jit(solution)/shard_map/all_to_all | solution.py:313

commit v3 on v0

--- a/solution.py
+++ b/solution.py
@@ -155,36 +155,39 @@
     flat = jnp.transpose(heavy_block, (0, 2, 1, 3)).reshape(
         species_count * cell_count, x_extent_size, merged
     )
+    rows = species_count * cell_count
+    kernel_count = fourier_scattering_table.shape[0]
     plain = jnp.arange(x_extent_size, dtype=jnp.int32)
     x_cos, x_sin = tables(plain, velocity_index(plain, x_extent_size), x_extent_size)
     wide_cos, wide_sin = kron_tables(NVY)
-    rows = species_count * cell_count
-    x_real = jnp.einsum("kp,bpm->kbm", x_cos, flat, precision=hp)
-    x_imag = -jnp.einsum("kp,bpm->kbm", x_sin, flat, precision=hp)
-    stacked = jnp.concatenate([x_real, x_imag], axis=1).reshape(-1, merged)
-    by_cos = split_dot(stacked, wide_cos).reshape(x_extent_size, 2, rows, merged)
-    by_sin = split_dot(stacked, wide_sin).reshape(x_extent_size, 2, rows, merged)
-    spec_real = by_cos[:, 0] + by_sin[:, 1]
-    spec_imag = by_cos[:, 1] - by_sin[:, 0]
-    kernels = jnp.transpose(fourier_scattering_table, (1, 0, 2))[:, :, None, :]
-    z_real = kernels * spec_real[:, None]
-    z_imag = kernels * spec_imag[:, None]
-    u_real = jnp.einsum("kp,kqbm->pqbm", x_cos, z_real, precision=hp) - jnp.einsum(
-        "kp,kqbm->pqbm", x_sin, z_imag, precision=hp
-    )
-    u_imag = jnp.einsum("kp,kqbm->pqbm", x_sin, z_real, precision=hp) + jnp.einsum(
-        "kp,kqbm->pqbm", x_cos, z_imag, precision=hp
+    square = (x_extent_size, x_extent_size)
+    fwd_cos = jnp.broadcast_to(x_cos, (rows,) + square)
+    fwd_sin = jnp.broadcast_to(x_sin, (rows,) + square)
+    x_real = jnp.einsum("bkp,bpm->bkm", fwd_cos, flat, precision=hp)
+    x_imag = -jnp.einsum("bkp,bpm->bkm", fwd_sin, flat, precision=hp)
+    stacked = jnp.concatenate([x_real, x_imag], axis=0).reshape(-1, merged)
+    by_cos = split_dot(stacked, wide_cos).reshape(2, rows, x_extent_size, merged)
+    by_sin = split_dot(stacked, wide_sin).reshape(2, rows, x_extent_size, merged)
+    spec_real = by_cos[0] + by_sin[1]
+    spec_imag = by_cos[1] - by_sin[0]
+    kernels = fourier_scattering_table[:, None]
+    z_real = kernels * spec_real[None]
+    z_imag = kernels * spec_imag[None]
+    inv_cos = jnp.broadcast_to(x_cos.T, (kernel_count, rows) + square)
+    inv_sin = jnp.broadcast_to(x_sin.T, (kernel_count, rows) + square)
+    u_real = jnp.einsum("qbpk,qbkm->qbpm", inv_cos, z_real, precision=hp) - jnp.einsum(
+        "qbpk,qbkm->qbpm", inv_sin, z_imag, precision=hp
+    )
+    u_imag = jnp.einsum("qbpk,qbkm->qbpm", inv_sin, z_real, precision=hp) + jnp.einsum(
+        "qbpk,qbkm->qbpm", inv_cos, z_imag, precision=hp
     )
     parts = (
         split_dot(u_real.reshape(-1, merged), wide_cos)
         - split_dot(u_imag.reshape(-1, merged), wide_sin)
-    ).reshape(
-        x_extent_size, fourier_scattering_table.shape[0], rows, merged
-    ) / (NVX * NVY * NVZ)
-    fields = jnp.transpose(flat, (1, 0, 2))
-    updated = fields + COLLIDE_SCALE * (parts[:, 0] * parts[:, 1] - fields * parts[:, 2])
+    ).reshape(kernel_count, rows, x_extent_size, merged) / (NVX * NVY * NVZ)
+    updated = flat + COLLIDE_SCALE * (parts[0] * parts[1] - flat * parts[2])
     return jnp.transpose(
-        updated.reshape(x_extent_size, species_count, cell_count, merged), (1, 0, 2, 3)
+        updated.reshape(species_count, cell_count, x_extent_size, merged), (0, 2, 1, 3)
     )
 
 

time: 172 us -> 141 us (0.82)
  local copies, waits for them, and re-layouts: 27.6 us -> 11.2 us
  matrix products: 30.5 us -> 18.6 us
  other arithmetic: 6.18 us -> 3.83 us
    reshape x5 -> x0, local copies, waits for them, and re-layouts: 10.8 us -> none  [the longest x1 2.54 us: collide_kron(): u_imag.reshape(-1, merged)]
    dot_general x12, matrix products: 23.2 us -> 13.4 us  [dot(): return jnp.dot(left, right, preferred_element_type=jnp.float32)]
    dot_general x6, matrix products: 7.28 us -> 5.24 us  [the longest x1 1.08 us: collide_kron(): jnp.einsum('qbpk,qbkm->qbpm', inv_sin, z_real, precision=hp)]
    sub x1 -> x0, local copies, waits for them, and re-layouts: 1.98 us -> none  [collide_kron(): jnp.einsum('kp,kqbm->pqbm', x_cos, z_real, precision=hp)]
    add x1 -> x0, local copies, waits for them, and re-layouts: 1.96 us -> none  [collide_kron(): jnp.einsum('kp,kqbm->pqbm', x_sin, z_real, precision=hp)]
    unnamed x42 -> x24, local copies, waits for them, and re-layouts: 4.6 us -> 5.68 us
where the time goes in v3:
time: 141 us; the launch traced here: 140 us
  waiting for transfers between devices  36.7 us (26%)
  blocking collectives  36.6 us (26%)
  starting transfers between devices  32.4 us (23%)
  matrix products  18.6 us (13%)
  local copies, waits for them, and re-layouts  11.2 us (8%)
  other arithmetic  3.83 us (3%)
    all_to_all x1, blocking collectives, body(): lax.all_to_all(result, 'vel', split_axis=1, concat_axis=2, tiled=True)  36.6 us
    all_to_all x1, waiting for transfers between devices, body(): lax.all_to_all(shifted, 'vel', split_axis=2, concat_axis=1, tiled=True)  24 us
    ppermute x1, starting transfers between devices, extended(): after = lax.ppermute(initial, axis, down)  22.6 us
    dot_general x12, matrix products, dot(): return jnp.dot(left, right, preferred_element_type=jnp.float32)  13.4 us
    ppermute x1, waiting for transfers between devices, extended(): before = lax.ppermute(last, axis, up)  12.8 us
    all_to_all x1, starting transfers between devices, body(): lax.all_to_all(shifted, 'vel', split_axis=2, concat_axis=1, tiled=True)  7.87 us
    unnamed x24, local copies, waits for them, and re-layouts  5.68 us
  transfers between devices with their start and end apart: 3, of which 2 were waited for; matrix products, arithmetic and copies ran while one was open for 0% of the time, Pallas kernels for 0%

profile of v3, /device:TPU:24, one launch (start us, length us, event | category | flops | bytes accessed | tf_op | source)
XLA Modules:
  0.0 139.8 jit_solution(1952273510978864487)
XLA Ops:
  0.0 1.0 fusion.63
  1.0 22.6 %collective-permute-start = (f32[5,1,1,1024]{3,2,1,0:T(1,128)S(1)}, f32[5,1,1,1024]{3,2,1,0:T(1,128)S(1)}, u32[]{:S(2)}, u32[]{:S(2)}) collective-permute-start(f32[5,1,1,1024]{3,2,1,0:T(1,128)S(1)} %get-tuple-element.26), channel_id=1, source_target_pairs={{32,0},{64,32},{96,64},{128,96},{160,128},{192,160},{224,192},{256... | collective-permute-start | bytes 61448 | tf_op jit(solution)/shard_map/ppermute | solution.py:29
  23.7 1.9 %collective-permute-start.1 = (f32[5,1,1,1024]{3,2,1,0:T(1,128)S(1)}, f32[5,1,1,1024]{3,2,1,0:T(1,128)S(1)}, u32[]{:S(2)}, u32[]{:S(2)}) collective-permute-start(f32[5,1,1,1024]{3,2,1,0:T(1,128)S(1)} %get-tuple-element.27), channel_id=1, source_target_pairs={{0,32},{32,64},{64,96},{96,128},{128,160},{160,192},{192,224},{224... | collective-permute-start | bytes 61448 | tf_op jit(solution)/shard_map/ppermute | solution.py:28
  25.6 12.8 %collective-permute-done.1 = f32[5,1,1,1024]{3,2,1,0:T(1,128)S(1)} collective-permute-done((f32[5,1,1,1024]{3,2,1,0:T(1,128)S(1)}, f32[5,1,1,1024]{3,2,1,0:T(1,128)S(1)}, u32[]{:S(2)}, u32[]{:S(2)}) %collective-permute-start.1) | collective-permute-done | bytes 20512 | tf_op jit(solution)/shard_map/ppermute | solution.py:28
  38.4 1.9 %fusion.25 = f32[5,1,32,1024]{3,2,1,0:T(8,128)S(1)} fusion(f32[5,1,32,1024]{3,2,1,0:T(8,128)} %param.9, f32[5,1,1,1024]{3,2,1,0:T(1,128)S(1)} %collective-permute-done.1, f32[5,1,1,1024]{3,2,1,0:T(1,128)S(1)} %collective-permute-done, f32[]{:T(128)} %bitcast.1), kind=kLoop, calls=%fused_computation.34 | loop fusion | flops 819200 | bytes 1351684 | tf_op jit(solution)/shard_map/sub | solution.py:287
  40.3 1.5 %copy.50 = f32[5,1,32,1024]{3,1,0,2:T(1,128)} copy(f32[5,1,32,1024]{3,2,1,0:T(8,128)S(1)} %fusion.25) | data formatting | bytes 1310720 | tf_op jit(solution)/shard_map/sub | solution.py:287
  41.8 7.9 %all-to-all-start = ((f32[5,1,32,1024]{3,1,0,2:T(1,128)}), f32[5,1,32,1024]{3,1,0,2:T(1,128)S(1)}, u32[]{:S(2)}, u32[]{:S(2)}) async-start(f32[5,1,32,1024]{3,1,0,2:T(1,128)} %copy.50), calls=%async_computation | async-start | bytes 1310720 | tf_op jit(solution)/shard_map/all_to_all | solution.py:290
  50.2 24.0 %all-to-all-done = f32[5,1,32,1024]{3,1,0,2:T(1,128)S(1)} async-done(((f32[5,1,32,1024]{3,1,0,2:T(1,128)}), f32[5,1,32,1024]{3,1,0,2:T(1,128)S(1)}, u32[]{:S(2)}, u32[]{:S(2)}) %all-to-all-start) | async-done | bytes 655392 | tf_op jit(solution)/shard_map/all_to_all | solution.py:290
  74.4 0.8 rev.4
  76.6 1.4 copy-done.1
  78.0 1.5 %fusion.67 = f32[192,1024]{1,0:T(8,128)} fusion(bf16[192,1024]{1,0:T(8,128)(2,1)S(1)} %get-tuple-element.22, bf16[1024,1024]{1,0:T(8,128)(2,1)S(1)} %copy-done.1), kind=kOutput, calls=%fused_computation.116 | convolution fusion | flops 402653184 | bytes 3276800 | tf_op jit(solution)/shard_map/dot_general | solution.py:147
  79.6 1.5 %fusion.65 = f32[192,1024]{1,0:T(8,128)} fusion(bf16[192,1024]{1,0:T(8,128)(2,1)S(1)} %get-tuple-element.22, bf16[1024,1024]{1,0:T(8,128)(2,1)S(1)} %copy-done.4), kind=kOutput, calls=%fused_computation.114 | convolution fusion | flops 402653184 | bytes 3276800 | tf_op jit(solution)/shard_map/dot_general | solution.py:147
  81.1 1.5 %fusion.66 = f32[192,1024]{1,0:T(8,128)} fusion(bf16[192,1024]{1,0:T(8,128)(2,1)S(1)} %get-tuple-element.23, bf16[1024,1024]{1,0:T(8,128)(2,1)S(1)} %copy-done.1), kind=kOutput, calls=%fused_computation.115 | convolution fusion | flops 402653184 | bytes 3276800 | tf_op jit(solution)/shard_map/dot_general | solution.py:147
  82.6 1.5 %fusion.64 = f32[192,1024]{1,0:T(8,128)} fusion(bf16[192,1024]{1,0:T(8,128)(2,1)S(1)} %get-tuple-element.23, bf16[1024,1024]{1,0:T(8,128)(2,1)S(1)} %copy-done.4), kind=kOutput, calls=%fused_computation.113 | convolution fusion | flops 402653184 | bytes 3276800 | tf_op jit(solution)/shard_map/dot_general | solution.py:147
  84.8 2.1 %fusion.18 = f32[192,1024]{1,0:T(8,128)S(1)} fusion(f32[192,1024]{1,0:T(8,128)} %fusion.66, f32[192,1024]{1,0:T(8,128)} %fusion.67, bf16[192,1024]{1,0:T(8,128)(2,1)S(1)} %get-tuple-element.23, bf16[1024,1024]{1,0:T(8,128)(2,1)S(1)} %copy-done), kind=kOutput, calls=%fused_computation.21 | convolution fusion | flops 403046400 | bytes 4849664 | tf_op jit(solution)/shard_map/dot_general | solution.py:147
  87.2 0.6 fusion.19
  88.0 0.9 copy-done.6
  88.9 1.1 fusion
  90.0 1.1 fusion.2
  91.0 1.1 fusion.11
  92.3 1.4 %copy-done.2 = bf16[1024,1024]{1,0:T(8,128)(2,1)S(1)} copy-done((bf16[1024,1024]{1,0:T(8,128)(2,1)S(1)}, bf16[1024,1024]{1,0:T(8,128)(2,1)}, u32[]{:S(2)}) %copy-start.2) | copy-done | bytes 2097176
  93.7 0.8 fusion.71
  94.5 1.1 fusion.8
  95.8 1.4 %copy-done.5 = bf16[1024,1024]{1,0:T(8,128)(2,1)S(1)} copy-done((bf16[1024,1024]{1,0:T(8,128)(2,1)S(1)}, bf16[1024,1024]{1,0:T(8,128)(2,1)}, u32[]{:S(2)}) %copy-start.5) | copy-done | bytes 2097176
  97.2 0.8 fusion.69
  98.0 0.8 fusion.68
  98.8 0.8 fusion.70
  99.6 0.8 fusion.16
  100.4 0.8 fusion.17
  101.6 0.7 copy.52
  102.3 36.6 %all_to_all.24 = f32[5,32,1,1024]{3,2,0,1:T(1,128)S(1)} all-to-all(f32[5,32,1,1024]{3,2,0,1:T(1,128)S(1)} %copy.52), channel_id=1, replica_groups=mesh['space'=32,'vel'=32] {'vel'}, dimensions={1} | all-to-all | bytes 1310720 | tf_op jit(solution)/shard_map/all_to_all | solution.py:311
  138.9 1.0 copy.59
  (54 shorter events, 3.9 us)
Async XLA Ops:
  1.0 24.6 %collective-permute-start = (f32[5,1,1,1024]{3,2,1,0:T(1,128)S(1)}, f32[5,1,1,1024]{3,2,1,0:T(1,128)S(1)}, u32[]{:S(2)}, u32[]{:S(2)}) collective-permute-start(f32[5,1,1,1024]{3,2,1,0:T(1,128)S(1)} %get-tuple-element.26), channel_id=1, source_target_pairs={{32,0},{64,32},{96,64},{128,96},{160,128},{192,160},{224,192},{256... | collective-permute-start | bytes 61448 | tf_op jit(solution)/shard_map/ppermute | solution.py:29
  23.7 14.7 %collective-permute-start.1 = (f32[5,1,1,1024]{3,2,1,0:T(1,128)S(1)}, f32[5,1,1,1024]{3,2,1,0:T(1,128)S(1)}, u32[]{:S(2)}, u32[]{:S(2)}) collective-permute-start(f32[5,1,1,1024]{3,2,1,0:T(1,128)S(1)} %get-tuple-element.27), channel_id=1, source_target_pairs={{0,32},{32,64},{64,96},{96,128},{128,160},{160,192},{192,224},{224... | collective-permute-start | bytes 61448 | tf_op jit(solution)/shard_map/ppermute | solution.py:28
  40.2 9.7 %copy-start.10 = (f32[2]{0:T(128)S(1)}, f32[2]{0:T(128)}, u32[]{:S(2)}) copy-start(f32[2]{0:T(128)} %param.13) | copy-start | bytes 28
  40.3 9.7 %copy-start.9 = (f32[2]{0:T(128)S(1)}, f32[2]{0:T(128)}, u32[]{:S(2)}) copy-start(f32[2]{0:T(128)} %param.12) | copy-start | bytes 28
  40.3 9.7 %copy-start.11 = (f32[5]{0:T(128)S(1)}, f32[5]{0:T(128)}, u32[]{:S(2)}) copy-start(f32[5]{0:T(128)} %param.11) | copy-start | bytes 64
  41.8 32.3 %all-to-all-start = ((f32[5,1,32,1024]{3,1,0,2:T(1,128)}), f32[5,1,32,1024]{3,1,0,2:T(1,128)S(1)}, u32[]{:S(2)}, u32[]{:S(2)}) async-start(f32[5,1,32,1024]{3,1,0,2:T(1,128)} %copy.50), calls=%async_computation | async-start | bytes 1310720 | tf_op jit(solution)/shard_map/all_to_all | solution.py:290
  76.4 1.6 %copy-start.1 = (bf16[1024,1024]{1,0:T(8,128)(2,1)S(1)}, bf16[1024,1024]{1,0:T(8,128)(2,1)}, u32[]{:S(2)}) copy-start(bf16[1024,1024]{1,0:T(8,128)(2,1)} %constant.74.clone) | copy-start | bytes 6291460
  78.0 1.7 %copy-start.4 = (bf16[1024,1024]{1,0:T(8,128)(2,1)S(1)}, bf16[1024,1024]{1,0:T(8,128)(2,1)}, u32[]{:S(2)}) copy-start(bf16[1024,1024]{1,0:T(8,128)(2,1)} %constant.72.clone) | copy-start | bytes 6291460
  82.6 2.2 %copy-start = (bf16[1024,1024]{1,0:T(8,128)(2,1)S(1)}, bf16[1024,1024]{1,0:T(8,128)(2,1)}, u32[]{:S(2)}) copy-start(bf16[1024,1024]{1,0:T(8,128)(2,1)} %constant.75.clone) | copy-start | bytes 6291460
  84.7 2.2 %copy-start.3 = (bf16[1024,1024]{1,0:T(8,128)(2,1)S(1)}, bf16[1024,1024]{1,0:T(8,128)(2,1)}, u32[]{:S(2)}) copy-start(bf16[1024,1024]{1,0:T(8,128)(2,1)} %constant.73.clone) | copy-start | bytes 6291460
  84.8 2.2 %copy-start.7 = (f32[192,1024]{1,0:T(8,128)S(1)}, f32[192,1024]{1,0:T(8,128)}, u32[]{:S(2)}) copy-start(f32[192,1024]{1,0:T(8,128)} %fusion.65) | copy-start | bytes 2359300
  84.8 2.5 %copy-start.8 = (f32[192,1024]{1,0:T(8,128)S(1)}, f32[192,1024]{1,0:T(8,128)}, u32[]{:S(2)}) copy-start(f32[192,1024]{1,0:T(8,128)} %fusion.64) | copy-start | bytes 2359300
  87.9 1.0 copy-start.6
  92.1 1.6 %copy-start.2 = (bf16[1024,1024]{1,0:T(8,128)(2,1)S(1)}, bf16[1024,1024]{1,0:T(8,128)(2,1)}, u32[]{:S(2)}) copy-start(bf16[1024,1024]{1,0:T(8,128)(2,1)} %constant.74.clone) | copy-start | bytes 6291460
  95.6 1.6 %copy-start.5 = (bf16[1024,1024]{1,0:T(8,128)(2,1)S(1)}, bf16[1024,1024]{1,0:T(8,128)(2,1)}, u32[]{:S(2)}) copy-start(bf16[1024,1024]{1,0:T(8,128)(2,1)} %constant.72.clone) | copy-start | bytes 6291460

commit v4 on v3

--- a/solution.py
+++ b/solution.py
@@ -161,26 +161,34 @@
     x_cos, x_sin = tables(plain, velocity_index(plain, x_extent_size), x_extent_size)
     wide_cos, wide_sin = kron_tables(NVY)
     square = (x_extent_size, x_extent_size)
-    fwd_cos = jnp.broadcast_to(x_cos, (rows,) + square)
-    fwd_sin = jnp.broadcast_to(x_sin, (rows,) + square)
-    x_real = jnp.einsum("bkp,bpm->bkm", fwd_cos, flat, precision=hp)
-    x_imag = -jnp.einsum("bkp,bpm->bkm", fwd_sin, flat, precision=hp)
-    stacked = jnp.concatenate([x_real, x_imag], axis=0).reshape(-1, merged)
+    forward = jnp.concatenate([x_cos, -x_sin], axis=0)
+    spectrum_x = jnp.einsum(
+        "bjp,bpm->bjm", jnp.broadcast_to(forward, (rows,) + forward.shape), flat, precision=hp
+    )
+    stacked = jnp.transpose(
+        spectrum_x.reshape(rows, 2, x_extent_size, merged), (1, 0, 2, 3)
+    ).reshape(-1, merged)
     by_cos = split_dot(stacked, wide_cos).reshape(2, rows, x_extent_size, merged)
     by_sin = split_dot(stacked, wide_sin).reshape(2, rows, x_extent_size, merged)
     spec_real = by_cos[0] + by_sin[1]
     spec_imag = by_cos[1] - by_sin[0]
     kernels = fourier_scattering_table[:, None]
-    z_real = kernels * spec_real[None]
-    z_imag = kernels * spec_imag[None]
-    inv_cos = jnp.broadcast_to(x_cos.T, (kernel_count, rows) + square)
-    inv_sin = jnp.broadcast_to(x_sin.T, (kernel_count, rows) + square)
-    u_real = jnp.einsum("qbpk,qbkm->qbpm", inv_cos, z_real, precision=hp) - jnp.einsum(
-        "qbpk,qbkm->qbpm", inv_sin, z_imag, precision=hp
-    )
-    u_imag = jnp.einsum("qbpk,qbkm->qbpm", inv_sin, z_real, precision=hp) + jnp.einsum(
-        "qbpk,qbkm->qbpm", inv_cos, z_imag, precision=hp
-    )
+    z_both = jnp.concatenate([kernels * spec_real[None], kernels * spec_imag[None]], axis=2)
+    inverse = jnp.concatenate(
+        [
+            jnp.concatenate([x_cos.T, -x_sin.T], axis=1),
+            jnp.concatenate([x_sin.T, x_cos.T], axis=1),
+        ],
+        axis=0,
+    )
+    u_both = jnp.einsum(
+        "qbij,qbjm->qbim",
+        jnp.broadcast_to(inverse, (kernel_count, rows) + inverse.shape),
+        z_both,
+        precision=hp,
+    )
+    u_real = u_both[:, :, :x_extent_size]
+    u_imag = u_both[:, :, x_extent_size:]
     parts = (
         split_dot(u_real.reshape(-1, merged), wide_cos)
         - split_dot(u_imag.reshape(-1, merged), wide_sin)

time: 141 us -> 133 us (0.943)
  matrix products: 18.6 us -> 11.4 us
    dot_general x12, matrix products: 13.4 us -> 8.38 us  [dot(): return jnp.dot(left, right, preferred_element_type=jnp.float32)]
    dot_general x6 -> x2, matrix products: 5.24 us -> 3.03 us  [the longest x1 2.2 us: collide_kron(): jnp.einsum('qbij,qbjm->qbim', jnp.broadcast_to(inverse, (kernel_count, ro...]
    unnamed x24 -> x16, local copies, waits for them, and re-layouts: 5.68 us -> 4.4 us
where the time goes in v4:
time: 133 us; the launch traced here: 132 us
  waiting for transfers between devices  36.6 us (28%)
  blocking collectives  36.6 us (28%)
  starting transfers between devices  32.4 us (24%)
  matrix products  11.4 us (9%)
  local copies, waits for them, and re-layouts  10.3 us (8%)
  other arithmetic  4.22 us (3%)
    all_to_all x1, blocking collectives, body(): lax.all_to_all(result, 'vel', split_axis=1, concat_axis=2, tiled=True)  36.6 us
    all_to_all x1, waiting for transfers between devices, body(): lax.all_to_all(shifted, 'vel', split_axis=2, concat_axis=1, tiled=True)  23.8 us
    ppermute x1, starting transfers between devices, extended(): after = lax.ppermute(initial, axis, down)  22.6 us
    ppermute x1, waiting for transfers between devices, extended(): before = lax.ppermute(last, axis, up)  12.8 us
    dot_general x12, matrix products, dot(): return jnp.dot(left, right, preferred_element_type=jnp.float32)  8.38 us
    all_to_all x1, starting transfers between devices, body(): lax.all_to_all(shifted, 'vel', split_axis=2, concat_axis=1, tiled=True)  7.87 us
    unnamed x16, local copies, waits for them, and re-layouts  4.4 us
  transfers between devices with their start and end apart: 3, of which 2 were waited for; matrix products, arithmetic and copies ran while one was open for 0% of the time, Pallas kernels for 0%

profile of v4, /device:TPU:24, one launch (start us, length us, event | category | flops | bytes accessed | tf_op | source)
XLA Modules:
  0.0 131.9 jit_solution(17243765581300324003)
XLA Ops:
  0.0 1.0 fusion.41
  1.0 22.6 %collective-permute-start = (f32[5,1,1,1024]{3,2,1,0:T(1,128)S(1)}, f32[5,1,1,1024]{3,2,1,0:T(1,128)S(1)}, u32[]{:S(2)}, u32[]{:S(2)}) collective-permute-start(f32[5,1,1,1024]{3,2,1,0:T(1,128)S(1)} %get-tuple-element.28), channel_id=1, source_target_pairs={{32,0},{64,32},{96,64},{128,96},{160,128},{192,160},{224,192},{256... | collective-permute-start | bytes 61448 | tf_op jit(solution)/shard_map/ppermute | solution.py:29
  23.7 1.9 %collective-permute-start.1 = (f32[5,1,1,1024]{3,2,1,0:T(1,128)S(1)}, f32[5,1,1,1024]{3,2,1,0:T(1,128)S(1)}, u32[]{:S(2)}, u32[]{:S(2)}) collective-permute-start(f32[5,1,1,1024]{3,2,1,0:T(1,128)S(1)} %get-tuple-element.29), channel_id=1, source_target_pairs={{0,32},{32,64},{64,96},{96,128},{128,160},{160,192},{192,224},{224... | collective-permute-start | bytes 61448 | tf_op jit(solution)/shard_map/ppermute | solution.py:28
  25.6 12.8 %collective-permute-done.1 = f32[5,1,1,1024]{3,2,1,0:T(1,128)S(1)} collective-permute-done((f32[5,1,1,1024]{3,2,1,0:T(1,128)S(1)}, f32[5,1,1,1024]{3,2,1,0:T(1,128)S(1)}, u32[]{:S(2)}, u32[]{:S(2)}) %collective-permute-start.1) | collective-permute-done | bytes 20512 | tf_op jit(solution)/shard_map/ppermute | solution.py:28
  38.4 1.8 %fusion.15 = f32[5,1,32,1024]{3,2,1,0:T(8,128)S(1)} fusion(f32[5,1,32,1024]{3,2,1,0:T(8,128)} %param.9, f32[5,1,1,1024]{3,2,1,0:T(1,128)S(1)} %collective-permute-done.1, f32[5,1,1,1024]{3,2,1,0:T(1,128)S(1)} %collective-permute-done, f32[]{:T(128)} %bitcast.1), kind=kLoop, calls=%fused_computation.26 | loop fusion | flops 819200 | bytes 1351684 | tf_op jit(solution)/shard_map/sub | solution.py:295
  40.2 1.5 %copy.67 = f32[5,1,32,1024]{3,1,0,2:T(1,128)} copy(f32[5,1,32,1024]{3,2,1,0:T(8,128)S(1)} %fusion.15) | data formatting | bytes 1310720 | tf_op jit(solution)/shard_map/sub | solution.py:295
  41.7 7.9 %all-to-all-start = ((f32[5,1,32,1024]{3,1,0,2:T(1,128)}), f32[5,1,32,1024]{3,1,0,2:T(1,128)S(1)}, u32[]{:S(2)}, u32[]{:S(2)}) async-start(f32[5,1,32,1024]{3,1,0,2:T(1,128)} %copy.67), calls=%async_computation | async-start | bytes 1310720 | tf_op jit(solution)/shard_map/all_to_all | solution.py:298
  50.3 23.8 %all-to-all-done = f32[5,1,32,1024]{3,1,0,2:T(1,128)S(1)} async-done(((f32[5,1,32,1024]{3,1,0,2:T(1,128)}), f32[5,1,32,1024]{3,1,0,2:T(1,128)S(1)}, u32[]{:S(2)}, u32[]{:S(2)}) %all-to-all-start) | async-done | bytes 655392 | tf_op jit(solution)/shard_map/all_to_all | solution.py:298
  74.3 0.8 rev.4
  75.4 0.8 fusion.16
  76.4 0.6 copy-done.3
  77.0 0.6 fusion.42
  77.6 0.6 fusion.43
  78.2 1.0 copy-done.2
  79.2 0.6 fusion.44
  79.8 0.6 fusion.45
  80.4 1.0 copy-done.1
  81.4 0.6 fusion.9
  82.0 1.0 copy-done
  83.0 0.6 fusion.8
  83.7 0.9 copy-done.4
  84.9 2.2 %fusion = f32[3,3,64,1024]{3,2,1,0:T(8,128)S(1)} fusion(f32[3,3,32,1024]{3,2,1,0:T(8,128)S(1)} %get-tuple-element.31, f32[3,3,32,1024]{3,2,1,0:T(8,128)S(1)} %get-tuple-element.30, f32[64,64]{1,0:T(8,128)S(1)} %maximum_maximum_fusion), kind=kOutput, calls=%fused_computation | convolution fusion | flops 453574656 | bytes 4734976 | tf_op jit(solution)/shard_map/qbij,qbjm->qbim/dot_general | solution.py:184
  87.4 0.4 fusion.10
  87.8 0.8 fusion.46
  88.6 0.8 fusion.47
  89.4 0.8 fusion.48
  90.2 0.8 fusion.49
  90.9 0.8 fusion.6
  91.8 0.8 fusion.7
  93.7 0.7 copy.71
  94.3 36.6 %all_to_all.24 = f32[5,32,1,1024]{3,2,0,1:T(1,128)S(1)} all-to-all(f32[5,32,1,1024]{3,2,0,1:T(1,128)S(1)} %copy.71), channel_id=1, replica_groups=mesh['space'=32,'vel'=32] {'vel'}, dimensions={1} | all-to-all | bytes 1310720 | tf_op jit(solution)/shard_map/all_to_all | solution.py:319
  131.0 1.0 copy.78
  (46 shorter events, 2.9 us)
Async XLA Ops:
  1.0 24.6 %collective-permute-start = (f32[5,1,1,1024]{3,2,1,0:T(1,128)S(1)}, f32[5,1,1,1024]{3,2,1,0:T(1,128)S(1)}, u32[]{:S(2)}, u32[]{:S(2)}) collective-permute-start(f32[5,1,1,1024]{3,2,1,0:T(1,128)S(1)} %get-tuple-element.28), channel_id=1, source_target_pairs={{32,0},{64,32},{96,64},{128,96},{160,128},{192,160},{224,192},{256... | collective-permute-start | bytes 61448 | tf_op jit(solution)/shard_map/ppermute | solution.py:29
  23.7 14.7 %collective-permute-start.1 = (f32[5,1,1,1024]{3,2,1,0:T(1,128)S(1)}, f32[5,1,1,1024]{3,2,1,0:T(1,128)S(1)}, u32[]{:S(2)}, u32[]{:S(2)}) collective-permute-start(f32[5,1,1,1024]{3,2,1,0:T(1,128)S(1)} %get-tuple-element.29), channel_id=1, source_target_pairs={{0,32},{32,64},{64,96},{96,128},{128,160},{160,192},{192,224},{224... | collective-permute-start | bytes 61448 | tf_op jit(solution)/shard_map/ppermute | solution.py:28
  38.4 11.8 %copy-start.6 = (f32[5]{0:T(128)S(1)}, f32[5]{0:T(128)}, u32[]{:S(2)}) copy-start(f32[5]{0:T(128)} %param.11) | copy-start | bytes 64
  38.4 11.9 %copy-start.7 = (f32[2]{0:T(128)S(1)}, f32[2]{0:T(128)}, u32[]{:S(2)}) copy-start(f32[2]{0:T(128)} %param.13) | copy-start | bytes 28
  38.4 11.9 %copy-start.5 = (f32[2]{0:T(128)S(1)}, f32[2]{0:T(128)}, u32[]{:S(2)}) copy-start(f32[2]{0:T(128)} %param.12) | copy-start | bytes 28
  41.7 32.3 %all-to-all-start = ((f32[5,1,32,1024]{3,1,0,2:T(1,128)}), f32[5,1,32,1024]{3,1,0,2:T(1,128)S(1)}, u32[]{:S(2)}, u32[]{:S(2)}) async-start(f32[5,1,32,1024]{3,1,0,2:T(1,128)} %copy.67), calls=%async_computation | async-start | bytes 1310720 | tf_op jit(solution)/shard_map/all_to_all | solution.py:298
  75.4 1.6 %copy-start.3 = (bf16[1024,1024]{1,0:T(8,128)(2,1)S(1)}, bf16[1024,1024]{1,0:T(8,128)(2,1)}, u32[]{:S(2)}) copy-start(bf16[1024,1024]{1,0:T(8,128)(2,1)} %constant.72.clone) | copy-start | bytes 6291460
  77.6 1.6 %copy-start.2 = (bf16[1024,1024]{1,0:T(8,128)(2,1)S(1)}, bf16[1024,1024]{1,0:T(8,128)(2,1)}, u32[]{:S(2)}) copy-start(bf16[1024,1024]{1,0:T(8,128)(2,1)} %constant.74.clone) | copy-start | bytes 6291460
  79.8 1.6 %copy-start.1 = (bf16[1024,1024]{1,0:T(8,128)(2,1)S(1)}, bf16[1024,1024]{1,0:T(8,128)(2,1)}, u32[]{:S(2)}) copy-start(bf16[1024,1024]{1,0:T(8,128)(2,1)} %constant.73.clone) | copy-start | bytes 6291460
  81.4 1.6 %copy-start = (bf16[1024,1024]{1,0:T(8,128)(2,1)S(1)}, bf16[1024,1024]{1,0:T(8,128)(2,1)}, u32[]{:S(2)}) copy-start(bf16[1024,1024]{1,0:T(8,128)(2,1)} %constant.75.clone) | copy-start | bytes 6291460
  83.6 1.0 copy-start.4

commit v5 on v4

--- a/solution.py
+++ b/solution.py
@@ -136,15 +136,17 @@
         low = (values - high.astype(np.float64)).astype(jnp.bfloat16)
         return jnp.asarray(high), jnp.asarray(low)
 
-    return split(np.cos(angles)), split(np.sin(angles))
-
-
-def split_dot(operand, table):
+    return split(np.concatenate([np.cos(angles), np.sin(angles)], axis=1))
+
+
+def split_dot(operand, table, table_dim=0):
     high, low = table
     op_high, op_low = split_bf16(operand)
 
     def dot(left, right):
-        return jnp.dot(left, right, preferred_element_type=jnp.float32)
+        return lax.dot_general(
+            left, right, (((1,), (table_dim,)), ((), ())), preferred_element_type=jnp.float32
+        )
 
     return dot(op_high, high) + (dot(op_low, high) + dot(op_high, low))
 
@@ -159,7 +161,7 @@
     kernel_count = fourier_scattering_table.shape[0]
     plain = jnp.arange(x_extent_size, dtype=jnp.int32)
     x_cos, x_sin = tables(plain, velocity_index(plain, x_extent_size), x_extent_size)
-    wide_cos, wide_sin = kron_tables(NVY)
+    wide = kron_tables(NVY)
     square = (x_extent_size, x_extent_size)
     forward = jnp.concatenate([x_cos, -x_sin], axis=0)
     spectrum_x = jnp.einsum(
@@ -168,8 +170,9 @@
     stacked = jnp.transpose(
         spectrum_x.reshape(rows, 2, x_extent_size, merged), (1, 0, 2, 3)
     ).reshape(-1, merged)
-    by_cos = split_dot(stacked, wide_cos).reshape(2, rows, x_extent_size, merged)
-    by_sin = split_dot(stacked, wide_sin).reshape(2, rows, x_extent_size, merged)
+    both = split_dot(stacked, wide)
+    by_cos = both[:, :merged].reshape(2, rows, x_extent_size, merged)
+    by_sin = both[:, merged:].reshape(2, rows, x_extent_size, merged)
     spec_real = by_cos[0] + by_sin[1]
     spec_imag = by_cos[1] - by_sin[0]
     kernels = fourier_scattering_table[:, None]
@@ -189,9 +192,9 @@
     )
     u_real = u_both[:, :, :x_extent_size]
     u_imag = u_both[:, :, x_extent_size:]
+    joined = jnp.concatenate([u_real, -u_imag], axis=3).reshape(-1, 2 * merged)
     parts = (
-        split_dot(u_real.reshape(-1, merged), wide_cos)
-        - split_dot(u_imag.reshape(-1, merged), wide_sin)
+        split_dot(joined, wide, table_dim=1)
     ).reshape(kernel_count, rows, x_extent_size, merged) / (NVX * NVY * NVZ)
     updated = flat + COLLIDE_SCALE * (parts[0] * parts[1] - flat * parts[2])
     return jnp.transpose(

time: 133 us -> 131 us (0.985)
  local copies, waits for them, and re-layouts: 10.3 us -> 8.83 us
    unnamed x16 -> x12, local copies, waits for them, and re-layouts: 4.4 us -> 3.25 us
    dot_general x12 -> x6, matrix products: 8.38 us -> 7.38 us  [dot(): lax.dot_general(left, right, (((1,), (table_dim,)), ((), ())), preferred_...]
where the time goes in v5:
time: 131 us; the launch traced here: 130 us
  waiting for transfers between devices  36.6 us (28%)
  blocking collectives  36.6 us (28%)
  starting transfers between devices  32.4 us (25%)
  matrix products  10.4 us (8%)
  local copies, waits for them, and re-layouts  8.83 us (7%)
  other arithmetic  4.57 us (3%)
    all_to_all x1, blocking collectives, body(): lax.all_to_all(result, 'vel', split_axis=1, concat_axis=2, tiled=True)  36.6 us
    all_to_all x1, waiting for transfers between devices, body(): lax.all_to_all(shifted, 'vel', split_axis=2, concat_axis=1, tiled=True)  23.8 us
    ppermute x1, starting transfers between devices, extended(): after = lax.ppermute(initial, axis, down)  22.6 us
    ppermute x1, waiting for transfers between devices, extended(): before = lax.ppermute(last, axis, up)  12.8 us
    all_to_all x1, starting transfers between devices, body(): lax.all_to_all(shifted, 'vel', split_axis=2, concat_axis=1, tiled=True)  7.87 us
    dot_general x6, matrix products, dot(): lax.dot_general(left, right, (((1,), (table_dim,)), ((), ())), preferred_...  7.38 us
    unnamed x12, local copies, waits for them, and re-layouts  3.25 us
  transfers between devices with their start and end apart: 3, of which 2 were waited for; matrix products, arithmetic and copies ran while one was open for 0% of the time, Pallas kernels for 0%

profile of v5, /device:TPU:24, one launch (start us, length us, event | category | flops | bytes accessed | tf_op | source)
XLA Modules:
  0.0 129.8 jit_solution(15911606747782424616)
XLA Ops:
  0.0 1.0 fusion.36
  1.0 22.6 %collective-permute-start = (f32[5,1,1,1024]{3,2,1,0:T(1,128)S(1)}, f32[5,1,1,1024]{3,2,1,0:T(1,128)S(1)}, u32[]{:S(2)}, u32[]{:S(2)}) collective-permute-start(f32[5,1,1,1024]{3,2,1,0:T(1,128)S(1)} %get-tuple-element.26), channel_id=1, source_target_pairs={{32,0},{64,32},{96,64},{128,96},{160,128},{192,160},{224,192},{256... | collective-permute-start | bytes 61448 | tf_op jit(solution)/shard_map/ppermute | solution.py:29
  23.7 1.9 %collective-permute-start.1 = (f32[5,1,1,1024]{3,2,1,0:T(1,128)S(1)}, f32[5,1,1,1024]{3,2,1,0:T(1,128)S(1)}, u32[]{:S(2)}, u32[]{:S(2)}) collective-permute-start(f32[5,1,1,1024]{3,2,1,0:T(1,128)S(1)} %get-tuple-element.27), channel_id=1, source_target_pairs={{0,32},{32,64},{64,96},{96,128},{128,160},{160,192},{192,224},{224... | collective-permute-start | bytes 61448 | tf_op jit(solution)/shard_map/ppermute | solution.py:28
  25.6 12.8 %collective-permute-done.1 = f32[5,1,1,1024]{3,2,1,0:T(1,128)S(1)} collective-permute-done((f32[5,1,1,1024]{3,2,1,0:T(1,128)S(1)}, f32[5,1,1,1024]{3,2,1,0:T(1,128)S(1)}, u32[]{:S(2)}, u32[]{:S(2)}) %collective-permute-start.1) | collective-permute-done | bytes 20512 | tf_op jit(solution)/shard_map/ppermute | solution.py:28
  38.4 1.8 %fusion.10 = f32[5,1,32,1024]{3,2,1,0:T(8,128)S(1)} fusion(f32[5,1,32,1024]{3,2,1,0:T(8,128)} %param.7, f32[5,1,1,1024]{3,2,1,0:T(1,128)S(1)} %collective-permute-done.1, f32[5,1,1,1024]{3,2,1,0:T(1,128)S(1)} %collective-permute-done, f32[]{:T(128)} %bitcast.1), kind=kLoop, calls=%fused_computation.20 | loop fusion | flops 819200 | bytes 1351684 | tf_op jit(solution)/shard_map/sub | solution.py:298
  40.2 1.5 %copy.65 = f32[5,1,32,1024]{3,1,0,2:T(1,128)} copy(f32[5,1,32,1024]{3,2,1,0:T(8,128)S(1)} %fusion.10) | data formatting | bytes 1310720 | tf_op jit(solution)/shard_map/sub | solution.py:298
  41.8 7.9 %all-to-all-start = ((f32[5,1,32,1024]{3,1,0,2:T(1,128)}), f32[5,1,32,1024]{3,1,0,2:T(1,128)S(1)}, u32[]{:S(2)}, u32[]{:S(2)}) async-start(f32[5,1,32,1024]{3,1,0,2:T(1,128)} %copy.65), calls=%async_computation | async-start | bytes 1310720 | tf_op jit(solution)/shard_map/all_to_all | solution.py:301
  49.7 0.2 fusion.31
  50.3 23.8 %all-to-all-done = f32[5,1,32,1024]{3,1,0,2:T(1,128)S(1)} async-done(((f32[5,1,32,1024]{3,1,0,2:T(1,128)}), f32[5,1,32,1024]{3,1,0,2:T(1,128)S(1)}, u32[]{:S(2)}, u32[]{:S(2)}) %all-to-all-start) | async-done | bytes 655392 | tf_op jit(solution)/shard_map/all_to_all | solution.py:301
  74.1 0.1 copy.77
  74.3 0.8 rev.4
  75.2 0.2 multiply_add_fusion
  75.4 0.8 fusion.11
  76.4 1.2 copy-done
  77.6 1.0 fusion.37
  78.6 1.2 copy-done.1
  79.8 1.0 convolution_add_fusion
  80.8 1.0 convolution_add_fusion.1
  82.0 0.9 copy-done.2
  82.9 0.3 broadcast_multiply_fusion.1
  83.2 2.2 %fusion.1 = f32[3,3,64,1024]{3,2,1,0:T(8,128)S(1)} fusion(f32[3,3,32,1024]{3,2,1,0:T(8,128)S(1)} %get-tuple-element.29, f32[3,3,32,1024]{3,2,1,0:T(8,128)S(1)} %get-tuple-element.28, f32[64,64]{1,0:T(8,128)S(1)} %maximum_maximum_fusion), kind=kOutput, calls=%fused_computation.5 | convolution fusion | flops 453574656 | bytes 4734976 | tf_op jit(solution)/shard_map/qbij,qbjm->qbim/dot_general | solution.py:187
  85.4 0.2 fusion.33
  85.6 0.2 pad_maximum_fusion
  85.9 0.3 fusion
  86.2 1.4 %fusion.38 = f32[288,1024]{1,0:T(8,128)S(1)} fusion(bf16[288,2048]{1,0:T(8,128)(2,1)S(1)} %get-tuple-element.15, bf16[1024,2048]{1,0:T(8,128)(2,1)S(1)} %copy-done), kind=kOutput, calls=%fused_computation.93 | convolution fusion | flops 1207959552 | bytes 6553600 | tf_op jit(solution)/shard_map/dot_general | solution.py:147
  87.6 1.4 %fusion.39 = f32[288,1024]{1,0:T(8,128)S(1)} fusion(bf16[288,2048]{1,0:T(8,128)(2,1)S(1)} %get-tuple-element.14, bf16[1024,2048]{1,0:T(8,128)(2,1)S(1)} %copy-done), kind=kOutput, calls=%fused_computation.94 | convolution fusion | flops 1207959552 | bytes 6553600 | tf_op jit(solution)/shard_map/dot_general | solution.py:147
  89.0 1.4 %fusion.6 = f32[288,1024]{1,0:T(8,128)S(1)} fusion(f32[288,1024]{1,0:T(8,128)S(1)} %fusion.38, f32[288,1024]{1,0:T(8,128)S(1)} %fusion.39, bf16[288,2048]{1,0:T(8,128)(2,1)S(1)} %get-tuple-element.15, bf16[1024,2048]{1,0:T(8,128)(2,1)S(1)} %copy-done.1), kind=kOutput, calls=%fused_computation.12 | convolution fusion | flops 1208844288 | bytes 8912896 | tf_op jit(solution)/shard_map/dot_general | solution.py:147
  90.6 0.2 slice_reduce_fusion
  90.8 0.2 exponential_reduce_fusion.2
  91.6 0.7 copy.69
  92.2 36.6 %all_to_all.24 = f32[5,32,1,1024]{3,2,0,1:T(1,128)S(1)} all-to-all(f32[5,32,1,1024]{3,2,0,1:T(1,128)S(1)} %copy.69), channel_id=1, replica_groups=mesh['space'=32,'vel'=32] {'vel'}, dimensions={1} | all-to-all | bytes 1310720 | tf_op jit(solution)/shard_map/all_to_all | solution.py:322
  128.8 1.0 copy.76
  (37 shorter events, 1.3 us)
Async XLA Ops:
  1.0 24.6 %collective-permute-start = (f32[5,1,1,1024]{3,2,1,0:T(1,128)S(1)}, f32[5,1,1,1024]{3,2,1,0:T(1,128)S(1)}, u32[]{:S(2)}, u32[]{:S(2)}) collective-permute-start(f32[5,1,1,1024]{3,2,1,0:T(1,128)S(1)} %get-tuple-element.26), channel_id=1, source_target_pairs={{32,0},{64,32},{96,64},{128,96},{160,128},{192,160},{224,192},{256... | collective-permute-start | bytes 61448 | tf_op jit(solution)/shard_map/ppermute | solution.py:29
  23.7 14.7 %collective-permute-start.1 = (f32[5,1,1,1024]{3,2,1,0:T(1,128)S(1)}, f32[5,1,1,1024]{3,2,1,0:T(1,128)S(1)}, u32[]{:S(2)}, u32[]{:S(2)}) collective-permute-start(f32[5,1,1,1024]{3,2,1,0:T(1,128)S(1)} %get-tuple-element.27), channel_id=1, source_target_pairs={{0,32},{32,64},{64,96},{96,128},{128,160},{160,192},{192,224},{224... | collective-permute-start | bytes 61448 | tf_op jit(solution)/shard_map/ppermute | solution.py:28
  40.2 10.0 %copy-start.4 = (f32[5]{0:T(128)S(1)}, f32[5]{0:T(128)}, u32[]{:S(2)}) copy-start(f32[5]{0:T(128)} %param.9) | copy-start | bytes 64
  40.2 10.0 %copy-start.5 = (f32[2]{0:T(128)S(1)}, f32[2]{0:T(128)}, u32[]{:S(2)}) copy-start(f32[2]{0:T(128)} %param.11) | copy-start | bytes 28
  40.2 10.0 %copy-start.3 = (f32[2]{0:T(128)S(1)}, f32[2]{0:T(128)}, u32[]{:S(2)}) copy-start(f32[2]{0:T(128)} %param.10) | copy-start | bytes 28
  41.8 32.3 %all-to-all-start = ((f32[5,1,32,1024]{3,1,0,2:T(1,128)}), f32[5,1,32,1024]{3,1,0,2:T(1,128)S(1)}, u32[]{:S(2)}, u32[]{:S(2)}) async-start(f32[5,1,32,1024]{3,1,0,2:T(1,128)} %copy.65), calls=%async_computation | async-start | bytes 1310720 | tf_op jit(solution)/shard_map/all_to_all | solution.py:301
  75.4 2.2 %copy-start = (bf16[1024,2048]{1,0:T(8,128)(2,1)S(1)}, bf16[1024,2048]{1,0:T(8,128)(2,1)}, u32[]{:S(2)}) copy-start(bf16[1024,2048]{1,0:T(8,128)(2,1)} %constant.68.clone) | copy-start | bytes 12582916
  77.6 2.2 %copy-start.1 = (bf16[1024,2048]{1,0:T(8,128)(2,1)S(1)}, bf16[1024,2048]{1,0:T(8,128)(2,1)}, u32[]{:S(2)}) copy-start(bf16[1024,2048]{1,0:T(8,128)(2,1)} %constant.69.clone) | copy-start | bytes 12582916
  81.9 1.0 copy-start.2

commit v6 on v5

--- a/solution.py
+++ b/solution.py
@@ -153,7 +153,7 @@
 
 def collide_kron(heavy_block, fourier_scattering_table):
     species_count, x_extent_size, cell_count, merged = heavy_block.shape
-    hp = lax.Precision.HIGHEST
+    hp = lax.Precision.HIGH
     flat = jnp.transpose(heavy_block, (0, 2, 1, 3)).reshape(
         species_count * cell_count, x_extent_size, merged
     )

time: 131 us -> 130 us (level)
  matrix products: 10.4 us -> 9.05 us
where the time goes in v6:
time: 130 us; the launch traced here: 129 us
  waiting for transfers between devices  36.6 us (28%)
  blocking collectives  36.6 us (28%)
  starting transfers between devices  32.4 us (25%)
  local copies, waits for them, and re-layouts  9.14 us (7%)
  matrix products  9.05 us (7%)
  other arithmetic  4.57 us (4%)
    all_to_all x1, blocking collectives, body(): lax.all_to_all(result, 'vel', split_axis=1, concat_axis=2, tiled=True)  36.6 us
    all_to_all x1, waiting for transfers between devices, body(): lax.all_to_all(shifted, 'vel', split_axis=2, concat_axis=1, tiled=True)  23.8 us
    ppermute x1, starting transfers between devices, extended(): after = lax.ppermute(initial, axis, down)  22.6 us
    ppermute x1, waiting for transfers between devices, extended(): before = lax.ppermute(last, axis, up)  12.8 us
    all_to_all x1, starting transfers between devices, body(): lax.all_to_all(shifted, 'vel', split_axis=2, concat_axis=1, tiled=True)  7.87 us
    dot_general x6, matrix products, dot(): lax.dot_general(left, right, (((1,), (table_dim,)), ((), ())), preferred_...  7.38 us
    unnamed x12, local copies, waits for them, and re-layouts  3.56 us
  transfers between devices with their start and end apart: 3, of which 2 were waited for; matrix products, arithmetic and copies ran while one was open for 0% of the time, Pallas kernels for 0%

profile of v6, /device:TPU:24, one launch (start us, length us, event | category | flops | bytes accessed | tf_op | source)
XLA Modules:
  0.0 128.7 jit_solution(15517507020540924003)
XLA Ops:
  0.0 1.0 fusion.36
  1.0 22.6 %collective-permute-start = (f32[5,1,1,1024]{3,2,1,0:T(1,128)S(1)}, f32[5,1,1,1024]{3,2,1,0:T(1,128)S(1)}, u32[]{:S(2)}, u32[]{:S(2)}) collective-permute-start(f32[5,1,1,1024]{3,2,1,0:T(1,128)S(1)} %get-tuple-element.26), channel_id=1, source_target_pairs={{32,0},{64,32},{96,64},{128,96},{160,128},{192,160},{224,192},{256... | collective-permute-start | bytes 61448 | tf_op jit(solution)/shard_map/ppermute | solution.py:29
  23.7 1.9 %collective-permute-start.1 = (f32[5,1,1,1024]{3,2,1,0:T(1,128)S(1)}, f32[5,1,1,1024]{3,2,1,0:T(1,128)S(1)}, u32[]{:S(2)}, u32[]{:S(2)}) collective-permute-start(f32[5,1,1,1024]{3,2,1,0:T(1,128)S(1)} %get-tuple-element.27), channel_id=1, source_target_pairs={{0,32},{32,64},{64,96},{96,128},{128,160},{160,192},{192,224},{224... | collective-permute-start | bytes 61448 | tf_op jit(solution)/shard_map/ppermute | solution.py:28
  25.6 12.8 %collective-permute-done.1 = f32[5,1,1,1024]{3,2,1,0:T(1,128)S(1)} collective-permute-done((f32[5,1,1,1024]{3,2,1,0:T(1,128)S(1)}, f32[5,1,1,1024]{3,2,1,0:T(1,128)S(1)}, u32[]{:S(2)}, u32[]{:S(2)}) %collective-permute-start.1) | collective-permute-done | bytes 20512 | tf_op jit(solution)/shard_map/ppermute | solution.py:28
  38.4 1.8 %fusion.10 = f32[5,1,32,1024]{3,2,1,0:T(8,128)S(1)} fusion(f32[5,1,32,1024]{3,2,1,0:T(8,128)} %param.7, f32[5,1,1,1024]{3,2,1,0:T(1,128)S(1)} %collective-permute-done.1, f32[5,1,1,1024]{3,2,1,0:T(1,128)S(1)} %collective-permute-done, f32[]{:T(128)} %bitcast.1), kind=kLoop, calls=%fused_computation.20 | loop fusion | flops 819200 | bytes 1351684 | tf_op jit(solution)/shard_map/sub | solution.py:298
  40.2 1.5 %copy.65 = f32[5,1,32,1024]{3,1,0,2:T(1,128)} copy(f32[5,1,32,1024]{3,2,1,0:T(8,128)S(1)} %fusion.10) | data formatting | bytes 1310720 | tf_op jit(solution)/shard_map/sub | solution.py:298
  41.8 7.9 %all-to-all-start = ((f32[5,1,32,1024]{3,1,0,2:T(1,128)}), f32[5,1,32,1024]{3,1,0,2:T(1,128)S(1)}, u32[]{:S(2)}, u32[]{:S(2)}) async-start(f32[5,1,32,1024]{3,1,0,2:T(1,128)} %copy.65), calls=%async_computation | async-start | bytes 1310720 | tf_op jit(solution)/shard_map/all_to_all | solution.py:301
  49.7 0.2 fusion.31
  50.3 23.8 %all-to-all-done = f32[5,1,32,1024]{3,1,0,2:T(1,128)S(1)} async-done(((f32[5,1,32,1024]{3,1,0,2:T(1,128)}), f32[5,1,32,1024]{3,1,0,2:T(1,128)S(1)}, u32[]{:S(2)}, u32[]{:S(2)}) %all-to-all-start) | async-done | bytes 655392 | tf_op jit(solution)/shard_map/all_to_all | solution.py:301
  74.1 0.1 copy.77
  74.3 0.8 rev.4
  75.2 0.2 multiply_add_fusion
  75.4 0.5 fusion.11
  76.1 1.5 %copy-done = bf16[1024,2048]{1,0:T(8,128)(2,1)S(1)} copy-done((bf16[1024,2048]{1,0:T(8,128)(2,1)S(1)}, bf16[1024,2048]{1,0:T(8,128)(2,1)}, u32[]{:S(2)}) %copy-start) | copy-done | bytes 4194328
  77.6 1.0 fusion.37
  78.6 1.2 copy-done.1
  79.8 1.0 convolution_add_fusion
  80.8 1.0 convolution_add_fusion.1
  82.0 0.9 copy-done.2
  82.9 0.3 broadcast_multiply_fusion.1
  83.2 1.2 fusion.1
  84.4 0.2 fusion.33
  84.5 0.2 pad_maximum_fusion
  84.8 0.3 fusion
  85.1 1.4 %fusion.38 = f32[288,1024]{1,0:T(8,128)S(1)} fusion(bf16[288,2048]{1,0:T(8,128)(2,1)S(1)} %get-tuple-element.15, bf16[1024,2048]{1,0:T(8,128)(2,1)S(1)} %copy-done), kind=kOutput, calls=%fused_computation.93 | convolution fusion | flops 1207959552 | bytes 6553600 | tf_op jit(solution)/shard_map/dot_general | solution.py:147
  86.6 1.4 %fusion.39 = f32[288,1024]{1,0:T(8,128)S(1)} fusion(bf16[288,2048]{1,0:T(8,128)(2,1)S(1)} %get-tuple-element.14, bf16[1024,2048]{1,0:T(8,128)(2,1)S(1)} %copy-done), kind=kOutput, calls=%fused_computation.94 | convolution fusion | flops 1207959552 | bytes 6553600 | tf_op jit(solution)/shard_map/dot_general | solution.py:147
  88.0 1.4 %fusion.6 = f32[288,1024]{1,0:T(8,128)S(1)} fusion(f32[288,1024]{1,0:T(8,128)S(1)} %fusion.38, f32[288,1024]{1,0:T(8,128)S(1)} %fusion.39, bf16[288,2048]{1,0:T(8,128)(2,1)S(1)} %get-tuple-element.15, bf16[1024,2048]{1,0:T(8,128)(2,1)S(1)} %copy-done.1), kind=kOutput, calls=%fused_computation.12 | convolution fusion | flops 1208844288 | bytes 8912896 | tf_op jit(solution)/shard_map/dot_general | solution.py:147
  89.5 0.2 slice_reduce_fusion
  89.7 0.2 exponential_reduce_fusion.2
  90.5 0.7 copy.69
  91.2 36.6 %all_to_all.24 = f32[5,32,1,1024]{3,2,0,1:T(1,128)S(1)} all-to-all(f32[5,32,1,1024]{3,2,0,1:T(1,128)S(1)} %copy.69), channel_id=1, replica_groups=mesh['space'=32,'vel'=32] {'vel'}, dimensions={1} | all-to-all | bytes 1310720 | tf_op jit(solution)/shard_map/all_to_all | solution.py:322
  127.8 1.0 copy.76
  (37 shorter events, 1.3 us)
Async XLA Ops:
  1.0 24.6 %collective-permute-start = (f32[5,1,1,1024]{3,2,1,0:T(1,128)S(1)}, f32[5,1,1,1024]{3,2,1,0:T(1,128)S(1)}, u32[]{:S(2)}, u32[]{:S(2)}) collective-permute-start(f32[5,1,1,1024]{3,2,1,0:T(1,128)S(1)} %get-tuple-element.26), channel_id=1, source_target_pairs={{32,0},{64,32},{96,64},{128,96},{160,128},{192,160},{224,192},{256... | collective-permute-start | bytes 61448 | tf_op jit(solution)/shard_map/ppermute | solution.py:29
  23.7 14.7 %collective-permute-start.1 = (f32[5,1,1,1024]{3,2,1,0:T(1,128)S(1)}, f32[5,1,1,1024]{3,2,1,0:T(1,128)S(1)}, u32[]{:S(2)}, u32[]{:S(2)}) collective-permute-start(f32[5,1,1,1024]{3,2,1,0:T(1,128)S(1)} %get-tuple-element.27), channel_id=1, source_target_pairs={{0,32},{32,64},{64,96},{96,128},{128,160},{160,192},{192,224},{224... | collective-permute-start | bytes 61448 | tf_op jit(solution)/shard_map/ppermute | solution.py:28
  40.2 10.0 %copy-start.4 = (f32[5]{0:T(128)S(1)}, f32[5]{0:T(128)}, u32[]{:S(2)}) copy-start(f32[5]{0:T(128)} %param.9) | copy-start | bytes 64
  40.2 10.0 %copy-start.5 = (f32[2]{0:T(128)S(1)}, f32[2]{0:T(128)}, u32[]{:S(2)}) copy-start(f32[2]{0:T(128)} %param.11) | copy-start | bytes 28
  40.2 10.0 %copy-start.3 = (f32[2]{0:T(128)S(1)}, f32[2]{0:T(128)}, u32[]{:S(2)}) copy-start(f32[2]{0:T(128)} %param.10) | copy-start | bytes 28
  41.8 32.3 %all-to-all-start = ((f32[5,1,32,1024]{3,1,0,2:T(1,128)}), f32[5,1,32,1024]{3,1,0,2:T(1,128)S(1)}, u32[]{:S(2)}, u32[]{:S(2)}) async-start(f32[5,1,32,1024]{3,1,0,2:T(1,128)} %copy.65), calls=%async_computation | async-start | bytes 1310720 | tf_op jit(solution)/shard_map/all_to_all | solution.py:301
  75.4 2.2 %copy-start = (bf16[1024,2048]{1,0:T(8,128)(2,1)S(1)}, bf16[1024,2048]{1,0:T(8,128)(2,1)}, u32[]{:S(2)}) copy-start(bf16[1024,2048]{1,0:T(8,128)(2,1)} %constant.68.clone) | copy-start | bytes 12582916
  77.6 2.2 %copy-start.1 = (bf16[1024,2048]{1,0:T(8,128)(2,1)S(1)}, bf16[1024,2048]{1,0:T(8,128)(2,1)}, u32[]{:S(2)}) copy-start(bf16[1024,2048]{1,0:T(8,128)(2,1)} %constant.69.clone) | copy-start | bytes 12582916
  81.9 1.0 copy-start.2
